TPU v7x, 32 devices: a whole 2x2x4 slice. The times are simulated.
32 devices in a mesh: ctx: 8 (over y, x, core), ch: 4 (over z).
Axes of the slice: x: 2, y: 2, z: 4, core: 2. Of those that a mesh axis runs over, the one named last changes fastest.
Arguments:
- query_one: bfloat16 [1024, 4096], P('ch', 'ctx'), may hold values from -6 to 6
- key_one: bfloat16 [1024, 4096], P('ch', 'ctx'), may hold values from -6 to 6
- value_one: bfloat16 [1024, 4096], P('ch', 'ctx'), may hold values from -6 to 6
- query_two: bfloat16 [1024, 4096], P('ch', 'ctx'), may hold values from -6 to 6
- key_two: bfloat16 [1024, 4096], P('ch', 'ctx'), may hold values from -6 to 6
- out_grad: bfloat16 [1024, 4096], P('ch', 'ctx'), may hold values from -6 to 6
- mr_filter: bfloat16 [64, 128], P('ch'), may hold values from -0.5 to 0.5
- li_rate: float32 [64, 16], P('ch'), may hold values from 3.6621094e-05 to 0.055
- li_residue: float32 [64, 16], P('ch'), may hold values from -1.5 to 1.5
- out_weight: bfloat16 [1024, 1024], P('ch'), may hold values from -0.1875 to 0.1875
Outputs:
- mixed: bfloat16 [1024, 4096], P('ch', 'ctx')
- query_one_grad: bfloat16 [1024, 4096], P('ch', 'ctx')
- key_one_grad: bfloat16 [1024, 4096], P('ch', 'ctx')
- value_one_grad: bfloat16 [1024, 4096], P('ch', 'ctx')
- query_two_grad: bfloat16 [1024, 4096], P('ch', 'ctx')
- key_two_grad: bfloat16 [1024, 4096], P('ch', 'ctx')
- weight_grad: float32 [1024, 1024], P('ch')
- filter_grad: float32 [64, 128], P('ch')
All inputs are finite; a program needn't handle non-finite values.
Results may differ from a plain program's by a relative error of at most 0.015.
Values may be sent and summed in bfloat16 or wider, within the bound.
No kernel may reach another device: no remote copies, remote signals or barrier semaphores. Data moves between devices by JAX's collectives and lax.ppermute only.
A program may use at most 128 MiB of HBM per device.

v0:
```python
import functools
import math

import jax
import jax.numpy as jnp
from jax import lax
from jax.experimental import pallas as pl
from jax.experimental.pallas import tpu as pltpu
from jax.sharding import PartitionSpec as P

BLK = 128
VMEM_LIMIT = 12 << 20
HIGHEST = lax.Precision.HIGHEST
F32 = jnp.float32
BF16 = jnp.bfloat16


def dot(a, b, ca=1, cb=0, precision=None):
    return lax.dot_general(
        a, b, (((ca,), (cb,)), ((), ())), preferred_element_type=F32, precision=precision
    )


def split(x):
    hi = x.astype(BF16)
    return hi, (x - hi.astype(F32)).astype(BF16)


def iota(shape, dim):
    return lax.broadcasted_iota(jnp.int32, shape, dim)


def rows_of(ref, g, size, first, count):
    return jnp.concatenate(
        [
            ref[g * size : (g + 1) * size, (first + b) * BLK : (first + b + 1) * BLK]
            for b in range(count)
        ],
        axis=0,
    )


def put_rows(ref, g, size, value):
    for b in range(value.shape[0] // size):
        ref[g * size : (g + 1) * size, b * BLK : (b + 1) * BLK] = value[
            b * size : (b + 1) * size
        ].astype(ref.dtype)


def circulant(row):
    return pltpu.roll(jnp.broadcast_to(row, (BLK, BLK)), 0, 1, stride=1, stride_axis=0)


def column(table):
    groups, modes = table.shape
    wide = jnp.broadcast_to(table[:, None, :], (groups, modes, modes)).reshape(-1, modes)
    diag = iota(wide.shape, 0) % modes == iota(wide.shape, 1)
    return jnp.sum(jnp.where(diag, wide, 0.0), axis=1, keepdims=True)


def meeting(rate, groups, modes):
    half = groups * modes
    hi, lo = split(jnp.exp(-column(rate) * (BLK - iota((half, BLK), 1).astype(F32))))
    return jnp.concatenate([hi, hi, lo], axis=0)


def per_channel(table, size):
    groups = table.shape[0]
    chans = groups * size
    pick = (iota((groups, chans), 1) // size == iota((groups, chans), 0)).astype(F32)
    return dot(table, pick, 0, 0, HIGHEST)


def block_states(table, stream, groups, modes, size):
    half = groups * modes
    chans = groups * size
    full = dot(table, stream, 1, 1)
    full = full[:half] + full[half:]
    own = iota((half, chans), 0) // modes == iota((half, chans), 1) // size
    return jnp.sum(jnp.where(own, full, 0.0).reshape(groups, modes, chans), axis=0)


def state_terms(states, table, groups, modes, size):
    chans = groups * size
    half = groups * modes
    count = len(states)
    hi, lo = split(jnp.concatenate(states, axis=1))
    pick = (iota((modes, half), 1) % modes == iota((modes, half), 0)).astype(BF16)
    own = (iota((count * chans, half), 0) % chans) // size == iota((count * chans, half), 1) // modes
    wide_hi = jnp.where(own, dot(hi, pick, 0, 0), 0.0).astype(BF16)
    wide_lo = jnp.where(own, dot(lo, pick, 0, 0), 0.0).astype(BF16)
    out = dot(jnp.concatenate([wide_hi, wide_lo, wide_hi], axis=1), table)
    return [out[i * chans : (i + 1) * chans] for i in range(count)]


def pack_rows(ref, d, first, value, width):
    half = value.shape[0] // 2
    for i, part in enumerate(split(value)):
        for j in range(2):
            at = (2 * i + j) * value.shape[1]
            ref[d, first:, at : at + value.shape[1]] = part[j * half : (j + 1) * half]
    if 4 * value.shape[1] < width:
        ref[d, first:, 4 * value.shape[1] :] = jnp.zeros((half, width - 4 * value.shape[1]), BF16)


def unpack_rows(ref, d, first, width):
    parts = [ref[d, first:, i * width : (i + 1) * width].astype(F32) for i in range(4)]
    return jnp.concatenate([parts[0] + parts[2], parts[1] + parts[3]], axis=0)


def tables_kernel(size, held, *refs):
    taps, rate, coef = refs[:3]
    sources = refs[3 : 3 + held]
    (short, long, close, open_, reach, rate_t, coef_t) = refs[3 + held : 10 + held]
    targets, sems = refs[10 + held : -1], refs[-1]
    copies = [
        pltpu.make_async_copy(source, target, sems.at[i])
        for i, (source, target) in enumerate(zip(sources, targets))
    ]
    for copy in copies:
        copy.start()
    groups, modes = rate.shape
    half = groups * modes
    col, coef_col = column(rate[...]), column(coef[...])
    at = iota((half, BLK), 1).astype(F32)
    falling = jnp.exp(-col * at)
    hi, lo = split(falling)
    open_[0:half] = hi
    open_[half:] = lo
    hi, lo = split(jnp.exp(-col * (BLK - 1.0 - at)))
    close[0:half] = hi
    close[half:] = lo
    hi, lo = split(jnp.exp(-col * (at + 1.0)))
    reach[0:half] = hi
    reach[half : 2 * half] = hi
    reach[2 * half :] = lo
    kernel = jnp.sum((coef_col * falling).reshape(groups, modes, BLK), axis=1)
    tap_rows = taps[...].astype(F32)
    later = iota((BLK, BLK), 1) >= iota((BLK, BLK), 0)
    for g in range(groups):
        turned = circulant(tap_rows[g : g + 1])
        short[g, 0:BLK] = jnp.where(later, 0.0, turned).astype(BF16)
        short[g, BLK:] = jnp.where(later, turned, 0.0).astype(BF16)
        long[g] = jnp.where(later, circulant(kernel[g : g + 1]), 0.0).astype(BF16)
    rate_t[...] = per_channel(rate[...], size)
    coef_t[...] = per_channel(coef[...], size)
    for copy in copies:
        copy.wait()


def first_kernel(
    size,
    halo,
    q1,
    k1,
    v1,
    k2,
    short,
    long,
    close,
    rate_t,
    conv,
    gated,
    local,
    mirrored,
    ahead,
    sub,
    sent,
    stream,
):
    groups = short.shape[0]
    modes = rate_t.shape[0]
    count = q1.shape[1] // BLK
    seen = jnp.where(lax.axis_index("ctx") > 0, halo[...], jnp.zeros(halo.shape, BF16))
    mirror = (iota((BLK, BLK), 1) + iota((BLK, BLK), 0) == BLK - 1).astype(BF16)
    for g in range(groups):
        rows = slice(g * size, (g + 1) * size)
        p1 = (rows_of(k1, g, size, 0, count).astype(F32) * rows_of(v1, g, size, 0, count).astype(F32)).astype(BF16)
        before = jnp.concatenate([seen[rows], p1[: (count - 1) * size]], axis=0)
        c1 = dot(jnp.concatenate([before, p1], axis=1), short[g])
        put_rows(conv, g, size, c1)
        g1 = (rows_of(q1, g, size, 0, count).astype(F32) * c1).astype(BF16)
        put_rows(gated, g, size, g1)
        p2 = (rows_of(k2, g, size, 0, count).astype(F32) * g1.astype(F32)).astype(BF16)
        put_rows(stream, g, size, p2)
        put_rows(local, g, size, dot(p2, long[g]))
    mirrored[:, :BLK] = dot(seen, mirror).astype(BF16)
    ahead[...] = (k2[:, :BLK].astype(F32) * q1[:, :BLK].astype(F32)).astype(BF16)
    for b in range(count):
        cols = slice(b * BLK, (b + 1) * BLK)
        p1 = (k1[:, cols].astype(F32) * v1[:, cols].astype(F32)).astype(BF16)
        mirrored[:, (b + 1) * BLK : (b + 2) * BLK] = dot(p1, mirror).astype(BF16)
    decay = jnp.exp(-rate_t[...] * BLK)
    total = None
    for b in range(count):
        state = block_states(close[...], stream[:, b * BLK : (b + 1) * BLK], groups, modes, size)
        sub[b] = state
        total = state if total is None else total * decay + state
    for d in range(sent.shape[0]):
        sent[d] = total


def second_kernel(
    size, groups, states, sub, rate_t, coef_t, reach, local, q2, weight, conv2, gated2, *parts
):
    modes = rate_t.shape[0]
    ctx_size, count = states.shape[0], sub.shape[0]
    length = float(count * BLK)
    me = lax.axis_index("ctx")
    rate = rate_t[...]
    entering = jnp.zeros(rate.shape, F32)
    for d in range(ctx_size):
        gap = me - 1 - d
        factor = jnp.exp(-rate * (length * jnp.maximum(gap, 0).astype(F32)))
        entering = entering + jnp.where(gap >= 0, factor * states[d], 0.0)
    decay = jnp.exp(-rate * BLK)
    coefs = coef_t[...]
    all_states = []
    for b in range(count):
        all_states.append(coefs * entering)
        entering = decay * entering + sub[b]
    terms = state_terms(all_states, reach[...], groups, modes, size)
    for b in range(count):
        cols = slice(b * BLK, (b + 1) * BLK)
        c2 = (local[:, cols].astype(F32) + terms[b]).astype(BF16)
        conv2[:, cols] = c2
        gated2[:, cols] = (q2[:, cols].astype(F32) * c2.astype(F32)).astype(BF16)
    here = lax.axis_index("ch")
    width = weight.shape[1] // len(parts)
    for k, part in enumerate(parts):
        at = pl.multiple_of(lax.rem(here + k, len(parts)) * width, BLK)
        part[...] = dot(weight[:, pl.ds(at, width)], gated2[...], 0, 0).astype(BF16)


def third_kernel(size, n_ch, fused, *refs):
    grads = refs[:n_ch]
    (weight, q2, conv2, gated2, long, open_, rate_t, coef_t, rate_g, ahead) = refs[n_ch : n_ch + 10]
    (q2_grad, local, sub, edge, sent, wsent, stream) = refs[n_ch + 10 :]
    groups = long.shape[0]
    modes, chans = rate_t.shape
    count = q2.shape[1] // BLK
    here = lax.axis_index("ch")
    width = weight.shape[1] // n_ch
    starts = [
        pl.multiple_of(lax.rem(here - k + n_ch, n_ch) * width, BLK) for k in range(n_ch)
    ]
    acc = None
    for k in range(n_ch):
        term = dot(weight[:, pl.ds(starts[k], width)], grads[k][...])
        acc = term if acc is None else acc + term
    q2_grad[...] = (acc * conv2[...].astype(F32)).astype(BF16)
    stream[...] = (acc * q2[...].astype(F32)).astype(BF16)
    for g in range(groups):
        put_rows(local, g, size, dot(rows_of(stream, g, size, 0, count), long[g], 1, 1))
    decay = jnp.exp(-rate_t[...] * BLK)
    total, inner = None, None
    for b in reversed(range(count)):
        state = block_states(open_[...], stream[:, b * BLK : (b + 1) * BLK], groups, modes, size)
        sub[b] = state
        inner = total
        total = state if total is None else total * decay + state
    meet = meeting(rate_g[...], groups, modes)
    (term,) = state_terms([coef_t[...] * inner], meet, groups, modes, size)
    edge[:, :BLK] = (local[:, :BLK].astype(F32) + term).astype(BF16)
    edge[:, BLK:] = ahead[...]
    if fused:
        rows = chans // sent.shape[0]
        for d in range(sent.shape[0]):
            pack_rows(sent, d, rows, total, sent.shape[2])
        wsent[...] = jnp.zeros(wsent.shape, wsent.dtype)
    else:
        for d in range(sent.shape[0]):
            sent[d] = total
    for k in range(n_ch):
        part = dot(gated2[...], grads[k][...], 1, 1)
        if fused:
            part = part.astype(BF16)
            for d in range(sent.shape[0]):
                sent[d, 0:rows, pl.ds(starts[k], width)] = part[d * rows : (d + 1) * rows]
        else:
            wsent[:, pl.ds(starts[k], width)] = part


def fourth_kernel(size, fused, states, edge, sub, rate_t, coef_t, rate_g, local, q1, k2, mirrored, p2_grad, turned_grad, out):
    modes, chans = rate_t.shape
    groups = chans // size
    count = sub.shape[0]
    length = float(count * BLK)
    ctx_size = states.shape[0]
    rows = chans // ctx_size
    me = lax.axis_index("ctx")
    rate = rate_t[...]
    coefs = coef_t[...]
    beyond = jnp.zeros(rate.shape, F32)
    following = jnp.zeros(rate.shape, F32)
    for d in range(ctx_size):
        if fused:
            state = unpack_rows(states, d, rows, chans)
        else:
            state = states[d]
        gap = d - me - 2
        factor = jnp.exp(-rate * (length * jnp.maximum(gap, 0).astype(F32)))
        beyond = beyond + jnp.where(gap >= 0, factor * state, 0.0)
        following = following + jnp.where(gap == -1, state, 0.0)
    decay = jnp.exp(-rate * BLK)
    entering = jnp.exp(-rate * length) * beyond + following
    all_states = [coefs * (jnp.exp(-rate * (length - BLK)) * beyond)]
    for b in reversed(range(count)):
        all_states.append(coefs * entering)
        entering = decay * entering + sub[b]
    terms = state_terms(all_states, meeting(rate_g[...], groups, modes), groups, modes, size)
    next_p = (edge[:, :BLK].astype(F32) + terms[0]).astype(BF16)
    beside = (next_p.astype(F32) * edge[:, BLK:].astype(F32)).astype(BF16)
    turned_grad[:, count * BLK :] = jnp.where(me < ctx_size - 1, beside, jnp.zeros(beside.shape, BF16))
    for b in range(count):
        cols = slice(b * BLK, (b + 1) * BLK)
        p2g = (local[:, cols].astype(F32) + terms[count - b]).astype(BF16)
        p2_grad[:, cols] = p2g
        g1g = p2g.astype(F32) * k2[:, cols].astype(F32)
        turned_grad[:, cols] = (g1g * q1[:, cols].astype(F32)).astype(BF16)
    later = iota((BLK, BLK), 1) + iota((BLK, BLK), 0) >= BLK - 1
    filters = []
    for g in range(groups):
        here = rows_of(turned_grad, g, size, 0, count)
        seen = rows_of(mirrored, g, size, 0, count + 1)
        inside = dot(seen[size:], here, 0, 0)
        across = dot(seen[: count * size], here, 0, 0)
        turned = pltpu.roll(jnp.where(later, inside, across), 1, 1, stride=1, stride_axis=0)
        filters.append(jnp.sum(turned, axis=0, keepdims=True))
    filter_rows = jnp.concatenate(filters, axis=0)
    if fused:
        total = states[0, 0:rows].astype(F32)
        for d in range(1, ctx_size):
            total = total + states[d, 0:rows].astype(F32)
        total = total.astype(BF16)
        for d in range(ctx_size):
            out[d, 0:rows] = total
            pack_rows(out, d, rows, filter_rows, out.shape[2])
    else:
        out[...] = filter_rows


def fifth_kernel(size, p2_grad, turned_grad, q2_grad, gated, conv, k2, k1, v1, short, q2_out, k2_out, q1_out, k1_out, v1_out):
    groups = short.shape[0]
    count = p2_grad.shape[1] // BLK
    q2_out[...] = q2_grad[...]
    p2g = p2_grad[...].astype(F32)
    k2_out[...] = (p2g * gated[...].astype(F32)).astype(BF16)
    q1_out[...] = (p2g * k2[...].astype(F32) * conv[...].astype(F32)).astype(BF16)
    for g in range(groups):
        kv, vv = rows_of(k1, g, size, 0, count).astype(F32), rows_of(v1, g, size, 0, count).astype(F32)
        here = rows_of(turned_grad, g, size, 0, count)
        after = rows_of(turned_grad, g, size, 1, count)
        p1g = dot(here, short[g, BLK:], 1, 1) + dot(after, short[g, 0:BLK], 1, 1)
        put_rows(k1_out, g, size, p1g * vv)
        put_rows(v1_out, g, size, p1g * kv)


def last_kernel(scale, moved, weight_out, filter_out):
    ctx_size, rows = weight_out.shape[:2]
    total = None
    for d in range(ctx_size):
        weight_out[d] = scale * moved[d, 0:rows].astype(F32)
        term = unpack_rows(moved, d, rows, BLK)
        total = term if total is None else total + term
    filter_out[...] = scale * total


def call(kernel, outs, *args, held=(), scratch=(), name):
    size = sum(math.prod(a.shape) * a.dtype.itemsize for a in args)
    size += sum(math.prod(s) * jnp.dtype(t).itemsize for s, t in outs)
    results = pl.pallas_call(
        kernel,
        out_shape=[
            pltpu.VMEM(s, t) if i in held else pltpu.HBM(s, t) for i, (s, t) in enumerate(outs)
        ],
        in_specs=[
            pl.BlockSpec(memory_space=pltpu.HBM if name == "tables" and i > 2 else pltpu.VMEM)
            for i in range(len(args))
        ],
        out_specs=[pl.BlockSpec(memory_space=pltpu.VMEM)] * len(outs),
        scratch_shapes=list(scratch),
        cost_estimate=pl.CostEstimate(flops=0, bytes_accessed=size, transcendentals=0),
        compiler_params=pltpu.CompilerParams(vmem_limit_bytes=VMEM_LIMIT),
    )(*args)
    return [
        pltpu.with_memory_space_constraint(o, pltpu.VMEM) if i in held else o
        for i, o in enumerate(results)
    ]


def around(count, step):
    return [(i, (i + step) % count) for i in range(count)]


def on_device(q1, k1, v1, q2, k2, out_grad, taps, rate, residue, weight):
    chans, length = q1.shape
    groups, _ = taps.shape
    modes = rate.shape[1]
    size = chans // groups
    half = groups * modes
    count = length // BLK
    n_ctx, n_ch = lax.axis_size("ctx"), lax.axis_size("ch")
    rows = chans // n_ctx
    fused = rows % 16 == 0 and groups == modes == 16 and 4 * chans == weight.shape[1]
    out_chans = weight.shape[1]
    width = out_chans // n_ch

    tail = (k1[:, length - BLK :].astype(F32) * v1[:, length - BLK :].astype(F32)).astype(BF16)
    halo = lax.ppermute(tail, "ctx", around(n_ctx, 1))
    grads = []
    for k in range(1, n_ch):
        grads.append(lax.ppermute(out_grad, "ch", around(n_ch, k)))

    coef = residue * jnp.sqrt(-jnp.expm1(-2.0 * rate))
    loaded = [
        pltpu.with_memory_space_constraint(a, pltpu.HBM)
        for a in (q1, k1, v1, q2, k2, out_grad, weight)
    ]
    late_q1, late_k1, late_v1, _, late_k2 = loaded[:5]
    short, long, close, open_, reach, rate_t, coef_t, q1, k1, v1, q2, k2, out_grad, weight = call(
        functools.partial(tables_kernel, size, len(loaded)),
        [
            ((groups, 2 * BLK, BLK), BF16),
            ((groups, BLK, BLK), BF16),
            ((2 * half, BLK), BF16),
            ((2 * half, BLK), BF16),
            ((3 * half, BLK), BF16),
            ((modes, chans), F32),
            ((modes, chans), F32),
        ]
        + [(a.shape, a.dtype) for a in loaded],
        taps,
        rate,
        coef,
        *loaded,
        held=range(14),
        scratch=[pltpu.SemaphoreType.DMA((len(loaded),))],
        name="tables",
    )
    stream = ((chans, length), BF16)
    blocks = ((count, modes, chans), F32)
    conv, gated, local, mirrored, ahead, sub, sent = call(
        functools.partial(first_kernel, size),
        [stream] * 3
        + [
            ((chans, length + BLK), BF16),
            ((chans, BLK), BF16),
            blocks,
            ((n_ctx, modes, chans), F32),
        ],
        halo,
        q1,
        k1,
        v1,
        k2,
        short,
        long,
        close,
        rate_t,
        held=range(7),
        scratch=[pltpu.VMEM((chans, length), BF16)],
        name="first",
    )
    states = lax.all_to_all(sent, "ctx", 0, 0, tiled=True)
    conv2, gated2, *parts = call(
        functools.partial(second_kernel, size, groups),
        [stream] * 2 + [((width, length), BF16)] * n_ch,
        states,
        sub,
        rate_t,
        coef_t,
        reach,
        local,
        q2,
        weight,
        held=range(2),
        name="second",
    )
    mixed_parts = [parts[0]]
    for k in range(1, n_ch):
        mixed_parts.append(lax.ppermute(parts[k], "ch", around(n_ch, k)))
    if fused:
        sent_shape, spare = ((n_ctx, rows + modes // 2, out_chans), BF16), ((8, BLK), F32)
    else:
        sent_shape, spare = ((n_ctx, modes, chans), F32), ((chans, out_chans), F32)
    q2_grad, local_back, sub_back, edge, sent_back, weight_part = call(
        functools.partial(third_kernel, size, n_ch, fused),
        [stream] * 2 + [blocks, ((chans, 2 * BLK), BF16), sent_shape, spare],
        out_grad,
        *grads,
        weight,
        q2,
        conv2,
        gated2,
        long,
        open_,
        rate_t,
        coef_t,
        rate,
        ahead,
        scratch=[pltpu.VMEM((chans, length), BF16)],
        name="third",
    )
    states_back = lax.all_to_all(sent_back, "ctx", 0, 0, tiled=True)
    next_edge = lax.ppermute(edge, "ctx", around(n_ctx, -1))
    p2_grad, turned_grad, last = call(
        functools.partial(fourth_kernel, size, fused),
        [stream, ((chans, length + BLK), BF16), sent_shape if fused else ((groups, BLK), F32)],
        states_back,
        next_edge,
        sub_back,
        rate_t,
        coef_t,
        rate,
        local_back,
        late_q1,
        late_k2,
        mirrored,
        name="fourth",
    )
    scale = 1.0 / math.sqrt(length * n_ctx)
    if fused:
        final = lax.all_to_all(last, "ctx", 0, 0, tiled=True)
    else:
        weight_total, filter_total = lax.psum((weight_part, last), "ctx")
    q2_out, k2_out, q1_out, k1_out, v1_out = call(
        functools.partial(fifth_kernel, size),
        [stream] * 5,
        p2_grad,
        turned_grad,
        q2_grad,
        gated,
        conv,
        late_k2,
        late_k1,
        late_v1,
        short,
        name="fifth",
    )
    mixed = sum(p.astype(F32) for p in mixed_parts).astype(BF16)
    if fused:
        weight_grad, filter_grad = call(
            functools.partial(last_kernel, scale),
            [((n_ctx, rows, out_chans), F32), ((groups, BLK), F32)],
            final,
            name="last",
        )
        weight_grad = weight_grad.reshape(chans, out_chans)
    else:
        weight_grad = scale * weight_total
        filter_grad = scale * filter_total
    return (mixed, q1_out, k1_out, v1_out, q2_out, k2_out, weight_grad, filter_grad)


def solution(mesh):
    cut, rows_only = P("ch", "ctx"), P("ch", None)

    return jax.shard_map(
        on_device,
        mesh=mesh,
        in_specs=(cut,) * 6 + (rows_only,) * 4,
        out_specs=(cut,) * 6 + (rows_only,) * 2,
        check_vma=False,
    )
```

profile of v0, /device:TPU:0, one launch (start us, length us, event | category | flops | bytes accessed | tf_op | source)
XLA Modules:
  0.0 85.3 jit_solution(12470470568710411862)
XLA Ops:
  0.6 0.0 copy-start.4
  0.6 0.0 copy-start.8
  0.7 3.1 %collective-permute-start.4 = (bf16[256,512]{1,0:T(8,128)(2,1)}, bf16[256,512]{1,0:T(8,128)(2,1)S(1)}, u32[]{:S(2)}, u32[]{:S(2)}) collective-permute-start(bf16[256,512]{1,0:T(8,128)(2,1)} %refs_8_.1), channel_id=1, source_target_pairs={{0,1},{1,2},{2,3},{3,0},{4,5},{5,6},{6,7},{7,4},{8,9},{9,10},{10,1... | collective-permute-start | bytes 786440 | tf_op jit(solution)/shard_map/ppermute | solution.py:413
  3.8 2.6 %collective-permute-start.5 = (bf16[256,512]{1,0:T(8,128)(2,1)}, bf16[256,512]{1,0:T(8,128)(2,1)S(1)}, u32[]{:S(2)}, u32[]{:S(2)}) collective-permute-start(bf16[256,512]{1,0:T(8,128)(2,1)} %refs_8_.1), channel_id=1, source_target_pairs={{0,2},{1,3},{2,0},{3,1},{4,6},{5,7},{6,4},{7,5},{8,10},{9,11},{10,... | collective-permute-start | bytes 786440 | tf_op jit(solution)/shard_map/ppermute | solution.py:413
  6.3 1.3 %collective-permute-start.6 = (bf16[256,512]{1,0:T(8,128)(2,1)}, bf16[256,512]{1,0:T(8,128)(2,1)S(1)}, u32[]{:S(2)}, u32[]{:S(2)}) collective-permute-start(bf16[256,512]{1,0:T(8,128)(2,1)} %refs_8_.1), channel_id=1, source_target_pairs={{0,3},{1,0},{2,1},{3,2},{4,7},{5,4},{6,5},{7,6},{8,11},{9,8},{10,9... | collective-permute-start | bytes 786440 | tf_op jit(solution)/shard_map/ppermute | solution.py:413
  7.7 0.9 %multiply_convert_fusion = bf16[256,128]{1,0:T(8,128)(2,1)S(1)} fusion(bf16[256,512]{1,0:T(8,128)(2,1)} %v1.1, bf16[256,512]{1,0:T(8,128)(2,1)} %k1.1), kind=kLoop, calls=%fused_computation.1 | loop fusion | flops 131072 | bytes 196608 | tf_op jit(solution)/shard_map/convert_element_type | solution.py:409
  8.6 0.0 copy-start.6
  8.6 0.1 collective-permute-start
  8.7 0.0 copy-done.4
  8.7 0.0 copy-done.8
  8.7 0.6 copy-done.6
  9.3 2.0 %shard_map.161 = (bf16[16,256,128]{2,1,0:T(8,128)(2,1)S(1)}, bf16[16,128,128]{2,1,0:T(8,128)(2,1)S(1)}, bf16[512,128]{1,0:T(8,128)(2,1)S(1)}, bf16[512,128]{1,0:...) custom-call(bf16[16,128]{1,0:T(8,128)(2,1)S(1)} %copy-done.6, ...), custom_call_target="tpu_custom_call" | custom-call | bytes 6264832 | tf_op jit(solution)/shard_map/pallas_call | solution.py:372
  11.3 1.9 %collective-permute-done.halo = bf16[256,128]{1,0:T(8,128)(2,1)S(1)} collective-permute-done((bf16[256,128]{1,0:T(8,128)(2,1)S(1)}, bf16[256,128]{1,0:T(8,128)(2,1)S(1)}, u32[]{:S(2)}, u32[]{:S(2)}) %collective-permute-start) | collective-permute-done | bytes 65568 | tf_op jit(solution)/shard_map/ppermute | solution.py:410
  13.2 0.9 %shard_map.162 = (bf16[256,512]{1,0:T(8,128)(2,1)S(1)}, bf16[256,512]{1,0:T(8,128)(2,1)S(1)}, bf16[256,512]{1,0:T(8,128)(2,1)S(1)}, bf16[256,640]{1,0:T(8,128)(2...) custom-call(bf16[256,128]{1,0:T(8,128)(2,1)S(1)} %collective-permute-done.halo, ...), custom_call_target="tpu_custom_call" | custom-call | bytes 4210688 | tf_op jit(solution)/shard_map/pallas_call | solution.py:372
  14.2 8.1 %all_to_all.15.states = f32[8,16,256]{2,1,0:T(8,128)S(1)} all-to-all(f32[8,16,256]{2,1,0:T(8,128)S(1)} %get-tuple-element.58), channel_id=1, replica_groups=mesh['ctx'=8,'ch'=4] {'ctx'}, dimensions={0} | all-to-all | bytes 262144 | tf_op jit(solution)/shard_map/all_to_all | solution.py:465
  22.3 2.3 %shard_map.163 = (bf16[256,512]{1,0:T(8,128)(2,1)S(1)}, bf16[256,512]{1,0:T(8,128)(2,1)S(1)}, bf16[256,512]{1,0:T(8,128)(2,1)}, bf16[256,512]{1,0:T(8,128)(2,1)}...) custom-call(f32[8,16,256]{2,1,0:T(8,128)S(1)} %all_to_all.15.states, f32[4,16,256]{2,1,0:T(8,128)S(1)} %get-tuple-element.59.sub, ...), custom_call_target="tpu_custom_call" | custom-call | bytes 3047424 | tf_op jit(solution)/shard_map/pallas_call | solution.py:372
  24.6 0.0 collective-permute-done.4.refs_1_
  24.6 0.0 collective-permute-done.5.refs_2_
  24.6 0.0 collective-permute-done.6.refs_3_
  24.6 2.8 %shard_map.164 = (bf16[256,512]{1,0:T(8,128)(2,1)}, bf16[256,512]{1,0:T(8,128)(2,1)}, f32[4,16,256]{2,1,0:T(8,128)}, bf16[256,256]{1,0:T(8,128)(2,1)}, bf16[8,40,1024]{2,1,0:T(8,128)(2,1)}, /*index=5*/f32[8,128]{1,0:T(8,128)}) custom-call(bf16[256,512]{1,0:T(8,128)(2,1)S(1)} %get-tuple-element.69.refs_0_, ...), custom_call_target="tpu_custom_call" | custom-call | bytes 4494336 | tf_op jit(solution)/shard_map/pallas_call | solution.py:372
  27.4 0.0 copy-start.12
  27.4 0.0 copy-start.3
  27.4 0.0 copy-start.5
  27.4 3.7 %all-to-all-start.1 = ((bf16[8,40,1024]{2,1,0:T(8,128)(2,1)}), bf16[8,40,1024]{2,1,0:T(8,128)(2,1)S(1)}, u32[]{:S(2)}, u32[]{:S(2)}) async-start(bf16[8,40,1024]{2,1,0:T(8,128)(2,1)} %get-tuple-element.74), calls=%async_computation.1 | async-start | bytes 1310720 | tf_op jit(solution)/shard_map/all_to_all | solution.py:505
  31.1 0.0 copy-done.12
  31.1 2.6 %collective-permute-start.7 = (bf16[256,256]{1,0:T(8,128)(2,1)S(1)}, bf16[256,256]{1,0:T(8,128)(2,1)S(1)}, u32[]{:S(2)}, u32[]{:S(2)}) collective-permute-start(bf16[256,256]{1,0:T(8,128)(2,1)S(1)} %copy-done.12), channel_id=1, source_target_pairs={{0,28},{4,0},{8,4},{12,8},{16,12},{20,16},{24,20},{28,24},{1,29},{... | collective-permute-start | bytes 393224 | tf_op jit(solution)/shard_map/ppermute | solution.py:506
  33.7 6.9 %collective-permute-done.7.edge = bf16[256,256]{1,0:T(8,128)(2,1)S(1)} collective-permute-done((bf16[256,256]{1,0:T(8,128)(2,1)S(1)}, bf16[256,256]{1,0:T(8,128)(2,1)S(1)}, u32[]{:S(2)}, u32[]{:S(2)}) %collective-permute-start.7) | collective-permute-done | bytes 131104 | tf_op jit(solution)/shard_map/ppermute | solution.py:506
  40.6 1.6 %all-to-all-done.1.states = bf16[8,40,1024]{2,1,0:T(8,128)(2,1)S(1)} async-done(((bf16[8,40,1024]{2,1,0:T(8,128)(2,1)}), bf16[8,40,1024]{2,1,0:T(8,128)(2,1)S(1)}, u32[]{:S(2)}, u32[]{:S(2)}) %all-to-all-start.1) | async-done | bytes 655392 | tf_op jit(solution)/shard_map/all_to_all | solution.py:505
  42.2 0.0 copy-done.3
  42.2 0.0 copy-done.5
  42.2 3.9 %shard_map.165 = (bf16[256,512]{1,0:T(8,128)(2,1)}, bf16[256,640]{1,0:T(8,128)(2,1)}, bf16[8,40,1024]{2,1,0:T(8,128)(2,1)}) custom-call(bf16[8,40,1024]{2,1,0:T(8,128)(2,1)S(1)} %all-to-all-done.1.states, bf16[256,256]{1,0:T(8,128)(2,1)S(1)} %collective-permute-done.7.edge, f32[4,16,256]{2,1,0:T(8,128)S(1)} %copy-done.5, ...), custom_call_target="tpu_custom_call" | custom-call | bytes 3245056 | tf_op jit(solution)/shard_map/pallas_call | solution.py:372
  46.0 0.0 copy-start.11
  46.1 0.0 copy-start.10
  46.1 0.0 copy-start.9
  46.1 0.0 copy-start.7
  46.1 3.7 %all-to-all-start.2 = ((bf16[8,40,1024]{2,1,0:T(8,128)(2,1)}), bf16[8,40,1024]{2,1,0:T(8,128)(2,1)S(1)}, u32[]{:S(2)}, u32[]{:S(2)}) async-start(bf16[8,40,1024]{2,1,0:T(8,128)(2,1)} %get-tuple-element.89), calls=%async_computation.2 | async-start | bytes 1310720 | tf_op jit(solution)/shard_map/all_to_all | solution.py:524
  49.8 0.0 copy-done.11
  49.8 6.4 %collective-permute-start.3 = (bf16[256,512]{1,0:T(8,128)(2,1)S(1)}, bf16[256,512]{1,0:T(8,128)(2,1)S(1)}, u32[]{:S(2)}, u32[]{:S(2)}) collective-permute-start(bf16[256,512]{1,0:T(8,128)(2,1)S(1)} %copy-done.11), channel_id=1, source_target_pairs={{0,3},{1,0},{2,1},{3,2},{4,7},{5,4},{6,5},{7,6},{8,11},{9,8},{10,9... | collective-permute-start | bytes 786440 | tf_op jit(solution)/shard_map/ppermute | solution.py:482
  56.2 0.0 copy-done.10
  56.2 0.4 collective-permute-start.2
  56.6 0.0 copy-done.9
  56.7 0.2 collective-permute-start.1
  56.9 6.1 %collective-permute-done.3 = bf16[256,512]{1,0:T(8,128)(2,1)S(1)} collective-permute-done((bf16[256,512]{1,0:T(8,128)(2,1)S(1)}, bf16[256,512]{1,0:T(8,128)(2,1)S(1)}, u32[]{:S(2)}, u32[]{:S(2)}) %collective-permute-start.3) | collective-permute-done | bytes 262176 | tf_op jit(solution)/shard_map/ppermute | solution.py:482
  63.0 17.0 %collective-permute-done.2 = bf16[256,512]{1,0:T(8,128)(2,1)S(1)} collective-permute-done((bf16[256,512]{1,0:T(8,128)(2,1)S(1)}, bf16[256,512]{1,0:T(8,128)(2,1)S(1)}, u32[]{:S(2)}, u32[]{:S(2)}) %collective-permute-start.2) | collective-permute-done | bytes 262176 | tf_op jit(solution)/shard_map/ppermute | solution.py:482
  80.0 0.0 collective-permute-done.1
  80.0 0.0 copy-done.7
  80.0 0.0 copy-start
  80.0 0.0 copy-start.1
  80.1 0.0 copy-start.2
  80.1 0.8 add_convert_fusion
  80.9 0.1 copy-done
  81.0 0.1 copy-done.1
  81.1 0.2 copy-done.2
  81.3 3.0 %shard_map.166 = (bf16[256,512]{1,0:T(8,128)(2,1)}, bf16[256,512]{1,0:T(8,128)(2,1)}, bf16[256,512]{1,0:T(8,128)(2,1)}, bf16[256,512]{1,0:T(8,128)(2,1)}, bf16[256,512]{1,0:T(8,128)(2,1)}) custom-call(bf16[256,512]{1,0:T(8,128)(2,1)S(1)} %copy-done.2, bf16[256,640]{1,0:T(8,128)(2,1)S(1)} %copy-done, bf16[256,512]{1,0:T(8,128)(2,1)S(1)} %copy-done.1, ...), custom_call_target="tpu_custom_call" | custom-call | bytes 4521984 | tf_op jit(solution)/shard_map/pallas_call | solution.py:372
  84.3 0.0 all-to-all-done.2.moved
  84.3 1.0 %shard_map.167 = (f32[8,32,1024]{2,1,0:T(8,128)}, f32[16,128]{1,0:T(8,128)}) custom-call(bf16[8,40,1024]{2,1,0:T(8,128)(2,1)S(1)} %all-to-all-done.2.moved), custom_call_target="tpu_custom_call" | custom-call | bytes 1712128 | tf_op jit(solution)/shard_map/pallas_call | solution.py:372
  (1 shorter events, 0.0 us)
Async XLA Ops:
  0.6 8.0 %copy-start.4 = (f32[16,16]{1,0:T(8,128)S(1)}, f32[16,16]{1,0:T(8,128)}, u32[]{:S(2)}) copy-start(f32[16,16]{1,0:T(8,128)} %rate_g.1) | copy-start | bytes 3076
  0.6 8.0 %copy-start.8 = (f32[16,16]{1,0:T(8,128)S(1)}, f32[16,16]{1,0:T(8,128)}, u32[]{:S(2)}) copy-start(f32[16,16]{1,0:T(8,128)} %param.18) | copy-start | bytes 3076
  0.7 24.0 %collective-permute-start.4 = (bf16[256,512]{1,0:T(8,128)(2,1)}, bf16[256,512]{1,0:T(8,128)(2,1)S(1)}, u32[]{:S(2)}, u32[]{:S(2)}) collective-permute-start(bf16[256,512]{1,0:T(8,128)(2,1)} %refs_8_.1), channel_id=1, source_target_pairs={{0,1},{1,2},{2,3},{3,0},{4,5},{5,6},{6,7},{7,4},{8,9},{9,10},{10,1... | collective-permute-start | bytes 786440 | tf_op jit(solution)/shard_map/ppermute | solution.py:413
  3.8 20.9 %collective-permute-start.5 = (bf16[256,512]{1,0:T(8,128)(2,1)}, bf16[256,512]{1,0:T(8,128)(2,1)S(1)}, u32[]{:S(2)}, u32[]{:S(2)}) collective-permute-start(bf16[256,512]{1,0:T(8,128)(2,1)} %refs_8_.1), channel_id=1, source_target_pairs={{0,2},{1,3},{2,0},{3,1},{4,6},{5,7},{6,4},{7,5},{8,10},{9,11},{10,... | collective-permute-start | bytes 786440 | tf_op jit(solution)/shard_map/ppermute | solution.py:413
  6.3 18.3 %collective-permute-start.6 = (bf16[256,512]{1,0:T(8,128)(2,1)}, bf16[256,512]{1,0:T(8,128)(2,1)S(1)}, u32[]{:S(2)}, u32[]{:S(2)}) collective-permute-start(bf16[256,512]{1,0:T(8,128)(2,1)} %refs_8_.1), channel_id=1, source_target_pairs={{0,3},{1,0},{2,1},{3,2},{4,7},{5,4},{6,5},{7,6},{8,11},{9,8},{10,9... | collective-permute-start | bytes 786440 | tf_op jit(solution)/shard_map/ppermute | solution.py:413
  8.6 0.7 copy-start.6
  8.6 4.6 %collective-permute-start = (bf16[256,128]{1,0:T(8,128)(2,1)S(1)}, bf16[256,128]{1,0:T(8,128)(2,1)S(1)}, u32[]{:S(2)}, u32[]{:S(2)}) collective-permute-start(bf16[256,128]{1,0:T(8,128)(2,1)S(1)} %multiply_convert_fusion), channel_id=1, source_target_pairs={{0,4},{4,8},{8,12},{12,16},{16,20},{20,24},{24,28},{28,0},{1,5},{5... | collective-permute-start | bytes 196616 | tf_op jit(solution)/shard_map/ppermute | solution.py:410
  27.4 3.7 %copy-start.12 = (bf16[256,256]{1,0:T(8,128)(2,1)S(1)}, bf16[256,256]{1,0:T(8,128)(2,1)}, u32[]{:S(2)}) copy-start(bf16[256,256]{1,0:T(8,128)(2,1)} %get-tuple-element.75) | copy-start | bytes 393220
  27.4 14.8 %copy-start.3 = (bf16[256,512]{1,0:T(8,128)(2,1)S(1)}, bf16[256,512]{1,0:T(8,128)(2,1)}, u32[]{:S(2)}) copy-start(bf16[256,512]{1,0:T(8,128)(2,1)} %get-tuple-element.77.local) | copy-start | bytes 786436
  27.4 14.8 %copy-start.5 = (f32[4,16,256]{2,1,0:T(8,128)S(1)}, f32[4,16,256]{2,1,0:T(8,128)}, u32[]{:S(2)}) copy-start(f32[4,16,256]{2,1,0:T(8,128)} %get-tuple-element.76.sub) | copy-start | bytes 196612
  27.4 14.7 %all-to-all-start.1 = ((bf16[8,40,1024]{2,1,0:T(8,128)(2,1)}), bf16[8,40,1024]{2,1,0:T(8,128)(2,1)S(1)}, u32[]{:S(2)}, u32[]{:S(2)}) async-start(bf16[8,40,1024]{2,1,0:T(8,128)(2,1)} %get-tuple-element.74), calls=%async_computation.1 | async-start | bytes 1310720 | tf_op jit(solution)/shard_map/all_to_all | solution.py:505
  31.1 9.5 %collective-permute-start.7 = (bf16[256,256]{1,0:T(8,128)(2,1)S(1)}, bf16[256,256]{1,0:T(8,128)(2,1)S(1)}, u32[]{:S(2)}, u32[]{:S(2)}) collective-permute-start(bf16[256,256]{1,0:T(8,128)(2,1)S(1)} %copy-done.12), channel_id=1, source_target_pairs={{0,28},{4,0},{8,4},{12,8},{16,12},{20,16},{24,20},{28,24},{1,29},{... | collective-permute-start | bytes 393224 | tf_op jit(solution)/shard_map/ppermute | solution.py:506
  46.0 3.7 %copy-start.11 = (bf16[256,512]{1,0:T(8,128)(2,1)S(1)}, bf16[256,512]{1,0:T(8,128)(2,1)}, u32[]{:S(2)}) copy-start(bf16[256,512]{1,0:T(8,128)(2,1)} %get-tuple-element.68) | copy-start | bytes 786436
  46.1 10.2 %copy-start.10 = (bf16[256,512]{1,0:T(8,128)(2,1)S(1)}, bf16[256,512]{1,0:T(8,128)(2,1)}, u32[]{:S(2)}) copy-start(bf16[256,512]{1,0:T(8,128)(2,1)} %get-tuple-element.67) | copy-start | bytes 786436
  46.1 10.6 %copy-start.9 = (bf16[256,512]{1,0:T(8,128)(2,1)S(1)}, bf16[256,512]{1,0:T(8,128)(2,1)}, u32[]{:S(2)}) copy-start(bf16[256,512]{1,0:T(8,128)(2,1)} %get-tuple-element.66) | copy-start | bytes 786436
  46.1 34.0 %copy-start.7 = (bf16[256,512]{1,0:T(8,128)(2,1)S(1)}, bf16[256,512]{1,0:T(8,128)(2,1)}, u32[]{:S(2)}) copy-start(bf16[256,512]{1,0:T(8,128)(2,1)} %get-tuple-element.65) | copy-start | bytes 786436
  46.1 38.2 %all-to-all-start.2 = ((bf16[8,40,1024]{2,1,0:T(8,128)(2,1)}), bf16[8,40,1024]{2,1,0:T(8,128)(2,1)S(1)}, u32[]{:S(2)}, u32[]{:S(2)}) async-start(bf16[8,40,1024]{2,1,0:T(8,128)(2,1)} %get-tuple-element.89), calls=%async_computation.2 | async-start | bytes 1310720 | tf_op jit(solution)/shard_map/all_to_all | solution.py:524
  49.8 13.2 %collective-permute-start.3 = (bf16[256,512]{1,0:T(8,128)(2,1)S(1)}, bf16[256,512]{1,0:T(8,128)(2,1)S(1)}, u32[]{:S(2)}, u32[]{:S(2)}) collective-permute-start(bf16[256,512]{1,0:T(8,128)(2,1)S(1)} %copy-done.11), channel_id=1, source_target_pairs={{0,3},{1,0},{2,1},{3,2},{4,7},{5,4},{6,5},{7,6},{8,11},{9,8},{10,9... | collective-permute-start | bytes 786440 | tf_op jit(solution)/shard_map/ppermute | solution.py:482
  56.2 23.8 %collective-permute-start.2 = (bf16[256,512]{1,0:T(8,128)(2,1)S(1)}, bf16[256,512]{1,0:T(8,128)(2,1)S(1)}, u32[]{:S(2)}, u32[]{:S(2)}) collective-permute-start(bf16[256,512]{1,0:T(8,128)(2,1)S(1)} %copy-done.10), channel_id=1, source_target_pairs={{0,2},{1,3},{2,0},{3,1},{4,6},{5,7},{6,4},{7,5},{8,10},{9,11},{10,... | collective-permute-start | bytes 786440 | tf_op jit(solution)/shard_map/ppermute | solution.py:482
  56.7 23.4 %collective-permute-start.1 = (bf16[256,512]{1,0:T(8,128)(2,1)S(1)}, bf16[256,512]{1,0:T(8,128)(2,1)S(1)}, u32[]{:S(2)}, u32[]{:S(2)}) collective-permute-start(bf16[256,512]{1,0:T(8,128)(2,1)S(1)} %copy-done.9), channel_id=1, source_target_pairs={{0,1},{1,2},{2,3},{3,0},{4,5},{5,6},{6,7},{7,4},{8,9},{9,10},{10,1... | collective-permute-start | bytes 786440 | tf_op jit(solution)/shard_map/ppermute | solution.py:482
  80.0 1.0 %copy-start = (bf16[256,640]{1,0:T(8,128)(2,1)S(1)}, bf16[256,640]{1,0:T(8,128)(2,1)}, u32[]{:S(2)}) copy-start(bf16[256,640]{1,0:T(8,128)(2,1)} %get-tuple-element.80.turned_grad) | copy-start | bytes 983044
  80.0 1.0 %copy-start.1 = (bf16[256,512]{1,0:T(8,128)(2,1)S(1)}, bf16[256,512]{1,0:T(8,128)(2,1)}, u32[]{:S(2)}) copy-start(bf16[256,512]{1,0:T(8,128)(2,1)} %get-tuple-element.81.q2_grad) | copy-start | bytes 786436
  80.1 1.2 %copy-start.2 = (bf16[256,512]{1,0:T(8,128)(2,1)S(1)}, bf16[256,512]{1,0:T(8,128)(2,1)}, u32[]{:S(2)}) copy-start(bf16[256,512]{1,0:T(8,128)(2,1)} %get-tuple-element.79.p2_grad) | copy-start | bytes 786436
where the time goes:
time: 85.8 us; the launch traced here: 85.3 us
  waiting for transfers between devices  33.6 us (39%)
  starting transfers between devices  24.1 us (28%)
  Pallas kernels  16 us (19%)
  blocking collectives  8.12 us (9%)
  other arithmetic  1.75 us (2%)
  local copies, waits for them, and re-layouts  0.97 us (1%)
    ppermute x3, waiting for transfers between devices, on_device(): mixed_parts.append(lax.ppermute(parts[k], 'ch', around(n_ch, k)))  23.2 us
    pallas_call x7, Pallas kernels, call(): pl.pallas_call(kernel, out_shape=[pltpu.VMEM(s, t) if i in held else pltp...  16 us
    all_to_all x1, blocking collectives, on_device(): states = lax.all_to_all(sent, 'ctx', 0, 0, tiled=True)  8.12 us
    ppermute x3, starting transfers between devices, on_device(): mixed_parts.append(lax.ppermute(parts[k], 'ch', around(n_ch, k)))  7.09 us
    ppermute x3, starting transfers between devices, on_device(): grads.append(lax.ppermute(out_grad, 'ch', around(n_ch, k)))  7.04 us
    ppermute x1, waiting for transfers between devices, on_device(): next_edge = lax.ppermute(edge, 'ctx', around(n_ctx, -1))  6.89 us
    all_to_all x1, starting transfers between devices, on_device(): states_back = lax.all_to_all(sent_back, 'ctx', 0, 0, tiled=True)  3.69 us
    all_to_all x1, starting transfers between devices, on_device(): final = lax.all_to_all(last, 'ctx', 0, 0, tiled=True)  3.69 us
  transfers between devices with their start and end apart: 10, of which 5 were waited for; matrix products, arithmetic and copies ran while one was open for 2% of the time, Pallas kernels for 10%

commit v1 on v0

--- a/solution.py
+++ b/solution.py
@@ -93,18 +93,19 @@
     return [out[i * chans : (i + 1) * chans] for i in range(count)]
 
 
-def pack_rows(ref, d, first, value, width):
-    half = value.shape[0] // 2
+def pack_rows(ref, first, value):
+    half, chans = value.shape[0] // 2, value.shape[1]
     for i, part in enumerate(split(value)):
         for j in range(2):
-            at = (2 * i + j) * value.shape[1]
-            ref[d, first:, at : at + value.shape[1]] = part[j * half : (j + 1) * half]
-    if 4 * value.shape[1] < width:
-        ref[d, first:, 4 * value.shape[1] :] = jnp.zeros((half, width - 4 * value.shape[1]), BF16)
-
-
-def unpack_rows(ref, d, first, width):
-    parts = [ref[d, first:, i * width : (i + 1) * width].astype(F32) for i in range(4)]
+            at = (2 * i + j) * chans
+            ref[first:, at : at + chans] = part[j * half : (j + 1) * half]
+    width = ref.shape[1]
+    if 4 * chans < width:
+        ref[first:, 4 * chans :] = jnp.zeros((half, width - 4 * chans), BF16)
+
+
+def unpack_rows(ref, first, chans):
+    parts = [ref[first:, i * chans : (i + 1) * chans].astype(F32) for i in range(4)]
     return jnp.concatenate([parts[0] + parts[2], parts[1] + parts[3]], axis=0)
 
 
@@ -232,10 +233,11 @@
         part[...] = dot(weight[:, pl.ds(at, width)], gated2[...], 0, 0).astype(BF16)
 
 
-def third_kernel(size, n_ch, fused, *refs):
+def third_kernel(size, n_ch, n_ctx, fused, *refs):
     grads = refs[:n_ch]
-    (weight, q2, conv2, gated2, long, open_, rate_t, coef_t, rate_g, ahead) = refs[n_ch : n_ch + 10]
-    (q2_grad, local, sub, edge, sent, wsent, stream) = refs[n_ch + 10 :]
+    (weight, q2, conv2, gated2, long, open_, rate_t) = refs[n_ch : n_ch + 7]
+    (q2_grad, local, sub, first, *sent) = refs[n_ch + 7 : -2]
+    whole, stream = refs[-2:]
     groups = long.shape[0]
     modes, chans = rate_t.shape
     count = q2.shape[1] // BLK
@@ -253,52 +255,60 @@
     for g in range(groups):
         put_rows(local, g, size, dot(rows_of(stream, g, size, 0, count), long[g], 1, 1))
     decay = jnp.exp(-rate_t[...] * BLK)
-    total, inner = None, None
+    total = None
     for b in reversed(range(count)):
         state = block_states(open_[...], stream[:, b * BLK : (b + 1) * BLK], groups, modes, size)
         sub[b] = state
-        inner = total
         total = state if total is None else total * decay + state
-    meet = meeting(rate_g[...], groups, modes)
-    (term,) = state_terms([coef_t[...] * inner], meet, groups, modes, size)
-    edge[:, :BLK] = (local[:, :BLK].astype(F32) + term).astype(BF16)
-    edge[:, BLK:] = ahead[...]
-    if fused:
-        rows = chans // sent.shape[0]
-        for d in range(sent.shape[0]):
-            pack_rows(sent, d, rows, total, sent.shape[2])
-        wsent[...] = jnp.zeros(wsent.shape, wsent.dtype)
-    else:
-        for d in range(sent.shape[0]):
-            sent[d] = total
+    first[...] = local[:, :BLK]
     for k in range(n_ch):
         part = dot(gated2[...], grads[k][...], 1, 1)
         if fused:
-            part = part.astype(BF16)
-            for d in range(sent.shape[0]):
-                sent[d, 0:rows, pl.ds(starts[k], width)] = part[d * rows : (d + 1) * rows]
+            whole[:, pl.ds(starts[k], width)] = part.astype(BF16)
         else:
-            wsent[:, pl.ds(starts[k], width)] = part
-
-
-def fourth_kernel(size, fused, states, edge, sub, rate_t, coef_t, rate_g, local, q1, k2, mirrored, p2_grad, turned_grad, out):
+            sent[1][:, pl.ds(starts[k], width)] = part
+    if fused:
+        rows = chans // n_ctx
+        me = lax.axis_index("ctx")
+        for k in range(n_ctx):
+            at = pl.multiple_of(jnp.bitwise_xor(me, k) * rows, rows)
+            sent[k][0:rows] = whole[pl.ds(at, rows), :]
+            pack_rows(sent[k], rows, total)
+    else:
+        for d in range(n_ctx):
+            sent[0][d] = total
+
+
+def between_kernel(size, local, sub, rate_t, coef_t, rate_g, ahead, edge):
+    modes, chans = rate_t.shape
+    count = sub.shape[0]
+    decay = jnp.exp(-rate_t[...] * BLK)
+    inner = sub[count - 1]
+    for b in reversed(range(1, count - 1)):
+        inner = inner * decay + sub[b]
+    meet = meeting(rate_g[...], chans // size, modes)
+    (term,) = state_terms([coef_t[...] * inner], meet, chans // size, modes, size)
+    edge[:, :BLK] = (local[...].astype(F32) + term).astype(BF16)
+    edge[:, BLK:] = ahead[...]
+
+
+def fourth_kernel(size, fused, n_ctx, *refs):
+    moved = refs[: n_ctx if fused else 1]
+    (sub, rate_t, coef_t, rate_g, local, q1, k2, mirrored) = refs[len(moved) : len(moved) + 8]
+    (beside, p2_grad, turned_grad, out) = refs[len(moved) + 8 :]
     modes, chans = rate_t.shape
     groups = chans // size
     count = sub.shape[0]
     length = float(count * BLK)
-    ctx_size = states.shape[0]
-    rows = chans // ctx_size
+    rows = chans // n_ctx
     me = lax.axis_index("ctx")
     rate = rate_t[...]
     coefs = coef_t[...]
     beyond = jnp.zeros(rate.shape, F32)
     following = jnp.zeros(rate.shape, F32)
-    for d in range(ctx_size):
-        if fused:
-            state = unpack_rows(states, d, rows, chans)
-        else:
-            state = states[d]
-        gap = d - me - 2
+    for k in range(n_ctx):
+        state = unpack_rows(moved[k], rows, chans) if fused else moved[0][k]
+        gap = (jnp.bitwise_xor(me, k) if fused else k) - me - 2
         factor = jnp.exp(-rate * (length * jnp.maximum(gap, 0).astype(F32)))
         beyond = beyond + jnp.where(gap >= 0, factor * state, 0.0)
         following = following + jnp.where(gap == -1, state, 0.0)
@@ -309,9 +319,7 @@
         all_states.append(coefs * entering)
         entering = decay * entering + sub[b]
     terms = state_terms(all_states, meeting(rate_g[...], groups, modes), groups, modes, size)
-    next_p = (edge[:, :BLK].astype(F32) + terms[0]).astype(BF16)
-    beside = (next_p.astype(F32) * edge[:, BLK:].astype(F32)).astype(BF16)
-    turned_grad[:, count * BLK :] = jnp.where(me < ctx_size - 1, beside, jnp.zeros(beside.shape, BF16))
+    beside[...] = terms[0]
     for b in range(count):
         cols = slice(b * BLK, (b + 1) * BLK)
         p2g = (local[:, cols].astype(F32) + terms[count - b]).astype(BF16)
@@ -329,46 +337,55 @@
         filters.append(jnp.sum(turned, axis=0, keepdims=True))
     filter_rows = jnp.concatenate(filters, axis=0)
     if fused:
-        total = states[0, 0:rows].astype(F32)
-        for d in range(1, ctx_size):
-            total = total + states[d, 0:rows].astype(F32)
-        total = total.astype(BF16)
-        for d in range(ctx_size):
-            out[d, 0:rows] = total
-            pack_rows(out, d, rows, filter_rows, out.shape[2])
+        total = moved[0][0:rows].astype(F32)
+        for k in range(1, n_ctx):
+            total = total + moved[k][0:rows].astype(F32)
+        out[0:rows] = total.astype(BF16)
+        pack_rows(out, rows, filter_rows)
     else:
         out[...] = filter_rows
 
 
-def fifth_kernel(size, p2_grad, turned_grad, q2_grad, gated, conv, k2, k1, v1, short, q2_out, k2_out, q1_out, k1_out, v1_out):
+def fifth_kernel(size, ctx_size, p2_grad, turned_grad, beside, edge, q2_grad, gated, conv, k2, k1, v1, short, q2_out, k2_out, q1_out, k1_out, v1_out, next_grad):
     groups = short.shape[0]
     count = p2_grad.shape[1] // BLK
     q2_out[...] = q2_grad[...]
     p2g = p2_grad[...].astype(F32)
     k2_out[...] = (p2g * gated[...].astype(F32)).astype(BF16)
     q1_out[...] = (p2g * k2[...].astype(F32) * conv[...].astype(F32)).astype(BF16)
+    next_p = (edge[:, :BLK].astype(F32) + beside[...]).astype(BF16)
+    near = (next_p.astype(F32) * edge[:, BLK:].astype(F32)).astype(BF16)
+    last = lax.axis_index("ctx") == ctx_size - 1
+    next_grad[...] = jnp.where(last, jnp.zeros(near.shape, BF16), near)
     for g in range(groups):
         kv, vv = rows_of(k1, g, size, 0, count).astype(F32), rows_of(v1, g, size, 0, count).astype(F32)
         here = rows_of(turned_grad, g, size, 0, count)
-        after = rows_of(turned_grad, g, size, 1, count)
+        after = jnp.concatenate([here[size:], next_grad[g * size : (g + 1) * size]], axis=0)
         p1g = dot(here, short[g, BLK:], 1, 1) + dot(after, short[g, 0:BLK], 1, 1)
         put_rows(k1_out, g, size, p1g * vv)
         put_rows(v1_out, g, size, p1g * kv)
 
 
-def last_kernel(scale, moved, weight_out, filter_out):
-    ctx_size, rows = weight_out.shape[:2]
+def last_kernel(scale, n_ctx, *refs):
+    moved, parts, (weight_out, filter_out, mixed) = refs[:n_ctx], refs[n_ctx:-3], refs[-3:]
+    rows = weight_out.shape[1]
+    me = lax.axis_index("ctx")
     total = None
-    for d in range(ctx_size):
-        weight_out[d] = scale * moved[d, 0:rows].astype(F32)
-        term = unpack_rows(moved, d, rows, BLK)
+    for k in range(n_ctx):
+        weight_out[jnp.bitwise_xor(me, k)] = scale * moved[k][0:rows].astype(F32)
+        term = unpack_rows(moved[k], rows, BLK)
         total = term if total is None else total + term
     filter_out[...] = scale * total
-
-
-def call(kernel, outs, *args, held=(), scratch=(), name):
+    summed = parts[0][...].astype(F32)
+    for part in parts[1:]:
+        summed = summed + part[...].astype(F32)
+    mixed[...] = summed.astype(BF16)
+
+
+def call(kernel, outs, *args, held=(), far=(), scratch=(), name):
     size = sum(math.prod(a.shape) * a.dtype.itemsize for a in args)
     size += sum(math.prod(s) * jnp.dtype(t).itemsize for s, t in outs)
+    args = [pltpu.with_memory_space_constraint(a, pltpu.HBM) if i in far else a for i, a in enumerate(args)]
     results = pl.pallas_call(
         kernel,
         out_shape=[
@@ -393,6 +410,22 @@
     return [(i, (i + step) % count) for i in range(count)]
 
 
+def exchange(blocks, count):
+    out = [blocks[0]]
+    for k in range(1, count):
+        out.append(lax.ppermute(blocks[k], "ctx", [(i, i ^ k) for i in range(count)]))
+    return out
+
+
+def gather(block, count):
+    out = {0: block}
+    for k in [1] + list(range(2, count, 2)):
+        out[k] = lax.ppermute(block, "ctx", [(i, i ^ k) for i in range(count)])
+    for k in range(2, count, 2):
+        out[k + 1] = lax.ppermute(out[k], "ctx", [(i, i ^ 1) for i in range(count)])
+    return [out[k] for k in range(count)]
+
+
 def on_device(q1, k1, v1, q2, k2, out_grad, taps, rate, residue, weight):
     chans, length = q1.shape
     groups, _ = taps.shape
@@ -403,6 +436,7 @@
     n_ctx, n_ch = lax.axis_size("ctx"), lax.axis_size("ch")
     rows = chans // n_ctx
     fused = rows % 16 == 0 and groups == modes == 16 and 4 * chans == weight.shape[1]
+    fused = fused and n_ctx & (n_ctx - 1) == 0
     out_chans = weight.shape[1]
     width = out_chans // n_ch
 
@@ -458,7 +492,7 @@
         long,
         close,
         rate_t,
-        held=range(7),
+        held=(2, 3, 5, 6),
         scratch=[pltpu.VMEM((chans, length), BF16)],
         name="first",
     )
@@ -480,13 +514,14 @@
     mixed_parts = [parts[0]]
     for k in range(1, n_ch):
         mixed_parts.append(lax.ppermute(parts[k], "ch", around(n_ch, k)))
+    packed = ((rows + modes // 2, out_chans), BF16)
     if fused:
-        sent_shape, spare = ((n_ctx, rows + modes // 2, out_chans), BF16), ((8, BLK), F32)
+        sent_shapes = [packed] * n_ctx
     else:
-        sent_shape, spare = ((n_ctx, modes, chans), F32), ((chans, out_chans), F32)
-    q2_grad, local_back, sub_back, edge, sent_back, weight_part = call(
-        functools.partial(third_kernel, size, n_ch, fused),
-        [stream] * 2 + [blocks, ((chans, 2 * BLK), BF16), sent_shape, spare],
+        sent_shapes = [((n_ctx, modes, chans), F32), ((chans, out_chans), F32)]
+    q2_grad, local_back, sub_back, first_back, *sent_back = call(
+        functools.partial(third_kernel, size, n_ch, n_ctx, fused),
+        [stream] * 2 + [blocks, ((chans, BLK), BF16)] + sent_shapes,
         out_grad,
         *grads,
         weight,
@@ -496,19 +531,30 @@
         long,
         open_,
         rate_t,
+        scratch=[pltpu.VMEM((chans, out_chans), BF16), pltpu.VMEM((chans, length), BF16)],
+        name="third",
+    )
+    if fused:
+        states_back = exchange(sent_back, n_ctx)
+    else:
+        states_back = [lax.all_to_all(sent_back[0], "ctx", 0, 0, tiled=True)]
+    (edge,) = call(
+        functools.partial(between_kernel, size),
+        [((chans, 2 * BLK), BF16)],
+        first_back,
+        sub_back,
+        rate_t,
         coef_t,
         rate,
         ahead,
-        scratch=[pltpu.VMEM((chans, length), BF16)],
-        name="third",
-    )
-    states_back = lax.all_to_all(sent_back, "ctx", 0, 0, tiled=True)
+        far=(0, 1, 5),
+        name="between",
+    )
     next_edge = lax.ppermute(edge, "ctx", around(n_ctx, -1))
-    p2_grad, turned_grad, last = call(
-        functools.partial(fourth_kernel, size, fused),
-        [stream, ((chans, length + BLK), BF16), sent_shape if fused else ((groups, BLK), F32)],
-        states_back,
-        next_edge,
+    beside, p2_grad, turned_grad, last = call(
+        functools.partial(fourth_kernel, size, fused, n_ctx),
+        [((chans, BLK), F32), stream, stream, packed if fused else ((groups, BLK), F32)],
+        *states_back,
         sub_back,
         rate_t,
         coef_t,
@@ -517,18 +563,21 @@
         late_q1,
         late_k2,
         mirrored,
+        far=(0, n_ctx) if fused else (),
         name="fourth",
     )
     scale = 1.0 / math.sqrt(length * n_ctx)
     if fused:
-        final = lax.all_to_all(last, "ctx", 0, 0, tiled=True)
+        final = gather(last, n_ctx)
     else:
-        weight_total, filter_total = lax.psum((weight_part, last), "ctx")
+        weight_total, filter_total = lax.psum((sent_back[1], last), "ctx")
     q2_out, k2_out, q1_out, k1_out, v1_out = call(
-        functools.partial(fifth_kernel, size),
+        functools.partial(fifth_kernel, size, n_ctx),
         [stream] * 5,
         p2_grad,
         turned_grad,
+        beside,
+        next_edge,
         q2_grad,
         gated,
         conv,
@@ -536,19 +585,22 @@
         late_k1,
         late_v1,
         short,
+        far=(0, 1, 2, 4, 5, 6),
+        scratch=[pltpu.VMEM((chans, BLK), BF16)],
         name="fifth",
     )
-    mixed = sum(p.astype(F32) for p in mixed_parts).astype(BF16)
     if fused:
-        weight_grad, filter_grad = call(
-            functools.partial(last_kernel, scale),
-            [((n_ctx, rows, out_chans), F32), ((groups, BLK), F32)],
-            final,
+        weight_grad, filter_grad, mixed = call(
+            functools.partial(last_kernel, scale, n_ctx),
+            [((n_ctx, rows, out_chans), F32), ((groups, BLK), F32), ((width, length), BF16)],
+            *final,
+            *mixed_parts,
             name="last",
         )
         weight_grad = weight_grad.reshape(chans, out_chans)
     else:
         weight_grad = scale * weight_total
+        mixed = sum(p.astype(F32) for p in mixed_parts).astype(BF16)
         filter_grad = scale * filter_total
     return (mixed, q1_out, k1_out, v1_out, q2_out, k2_out, weight_grad, filter_grad)
 

time: 85.8 us -> 67.3 us (0.78)
  waiting for transfers between devices: 33.6 us -> 17 us
  starting transfers between devices: 24.1 us -> 20.6 us
  Pallas kernels: 16 us -> 18.9 us
    ppermute x3, waiting for transfers between devices: 23.2 us -> 0.01 us  [on_device(): mixed_parts.append(lax.ppermute(parts[k], 'ch', around(n_ch, k)))]
    ppermute x0 -> x14, starting transfers between devices: none -> 13.2 us  [the longest x7 7.34 us: exchange(): lax.ppermute(blocks[k], 'ctx', [(i, i ^ k) for i in range(count)])]
    ppermute x0 -> x14, waiting for transfers between devices: none -> 10.1 us  [the longest x4 5.72 us: gather(): out[k] = lax.ppermute(block, 'ctx', [(i, i ^ k) for i in range(count)])]
    all_to_all x2 -> x0, starting transfers between devices: 7.37 us -> none  [the longest x1 3.69 us: on_device(): states_back = lax.all_to_all(sent_back, 'ctx', 0, 0, tiled=True)]
    ppermute x3, starting transfers between devices: 7.09 us -> 0.06 us  [on_device(): mixed_parts.append(lax.ppermute(parts[k], 'ch', around(n_ch, k)))]
    ppermute x1, waiting for transfers between devices: 6.89 us -> 0.01 us  [on_device(): next_edge = lax.ppermute(edge, 'ctx', around(n_ctx, -1))]
    ppermute x3, waiting for transfers between devices: 0.01 us -> 4.93 us  [on_device(): grads.append(lax.ppermute(out_grad, 'ch', around(n_ch, k)))]
    pallas_call x7 -> x8, Pallas kernels: 16 us -> 18.9 us  [call(): pl.pallas_call(kernel, out_shape=[pltpu.VMEM(s, t) if i in held else pltp...]
  transfers between devices with their start and end apart: 10 -> 22, of which waited for: 5 -> 5; matrix products, arithmetic and copies ran while one was open for 2% -> 1% of each run, Pallas kernels for 10% -> 23%
where the time goes in v1:
time: 67.3 us; the launch traced here: 66.9 us
  starting transfers between devices  20.6 us (31%)
  Pallas kernels  18.9 us (28%)
  waiting for transfers between devices  17 us (25%)
  blocking collectives  8.11 us (12%)
  other arithmetic  0.91 us (1%)
  between operations  0.82 us (1%)
    pallas_call x8, Pallas kernels, call(): pl.pallas_call(kernel, out_shape=[pltpu.VMEM(s, t) if i in held else pltp...  18.9 us
    all_to_all x1, blocking collectives, on_device(): states = lax.all_to_all(sent, 'ctx', 0, 0, tiled=True)  8.11 us
    ppermute x7, starting transfers between devices, exchange(): lax.ppermute(blocks[k], 'ctx', [(i, i ^ k) for i in range(count)])  7.34 us
    ppermute x3, starting transfers between devices, on_device(): grads.append(lax.ppermute(out_grad, 'ch', around(n_ch, k)))  6.14 us
    ppermute x4, waiting for transfers between devices, gather(): out[k] = lax.ppermute(block, 'ctx', [(i, i ^ k) for i in range(count)])  5.72 us
    ppermute x4, starting transfers between devices, gather(): out[k] = lax.ppermute(block, 'ctx', [(i, i ^ k) for i in range(count)])  5.28 us
    ppermute x3, waiting for transfers between devices, on_device(): grads.append(lax.ppermute(out_grad, 'ch', around(n_ch, k)))  4.93 us
    ppermute x7, waiting for transfers between devices, exchange(): lax.ppermute(blocks[k], 'ctx', [(i, i ^ k) for i in range(count)])  4.41 us
  transfers between devices with their start and end apart: 22, of which 5 were waited for; matrix products, arithmetic and copies ran while one was open for 1% of the time, Pallas kernels for 23%

profile of v1, /device:TPU:0, one launch (start us, length us, event | category | flops | bytes accessed | tf_op | source)
XLA Modules:
  0.0 66.9 jit_solution(13112911641297720843)
XLA Ops:
  0.6 0.0 copy-start.2
  0.6 0.0 copy-start.5
  0.7 3.1 %collective-permute-start = (bf16[256,512]{1,0:T(8,128)(2,1)}, bf16[256,512]{1,0:T(8,128)(2,1)S(1)}, u32[]{:S(2)}, u32[]{:S(2)}) collective-permute-start(bf16[256,512]{1,0:T(8,128)(2,1)} %refs_8_.1), channel_id=1, source_target_pairs={{0,1},{1,2},{2,3},{3,0},{4,5},{5,6},{6,7},{7,4},{8,9},{9,10},{10,1... | collective-permute-start | bytes 786440 | tf_op jit(solution)/shard_map/ppermute | solution.py:447
  3.8 2.1 %collective-permute-start.2 = (bf16[256,512]{1,0:T(8,128)(2,1)}, bf16[256,512]{1,0:T(8,128)(2,1)S(1)}, u32[]{:S(2)}, u32[]{:S(2)}) collective-permute-start(bf16[256,512]{1,0:T(8,128)(2,1)} %refs_8_.1), channel_id=1, source_target_pairs={{0,3},{1,0},{2,1},{3,2},{4,7},{5,4},{6,5},{7,6},{8,11},{9,8},{10,9... | collective-permute-start | bytes 786440 | tf_op jit(solution)/shard_map/ppermute | solution.py:447
  5.9 0.9 %collective-permute-start.1 = (bf16[256,512]{1,0:T(8,128)(2,1)}, bf16[256,512]{1,0:T(8,128)(2,1)S(1)}, u32[]{:S(2)}, u32[]{:S(2)}) collective-permute-start(bf16[256,512]{1,0:T(8,128)(2,1)} %refs_8_.1), channel_id=1, source_target_pairs={{0,2},{1,3},{2,0},{3,1},{4,6},{5,7},{6,4},{7,5},{8,10},{9,11},{10,... | collective-permute-start | bytes 786440 | tf_op jit(solution)/shard_map/ppermute | solution.py:447
  6.8 0.9 %multiply_convert_fusion = bf16[256,128]{1,0:T(8,128)(2,1)S(1)} fusion(bf16[256,512]{1,0:T(8,128)(2,1)} %v1.1, bf16[256,512]{1,0:T(8,128)(2,1)} %k1.1), kind=kLoop, calls=%fused_computation | loop fusion | flops 131072 | bytes 196608 | tf_op jit(solution)/shard_map/convert_element_type | solution.py:443
  7.7 0.0 copy-start.4
  7.7 0.1 collective-permute-start.3
  7.8 0.0 copy-done.2
  7.8 0.0 copy-done.5
  7.8 0.6 copy-done.4
  8.4 2.0 %shard_map.161 = (bf16[16,256,128]{2,1,0:T(8,128)(2,1)S(1)}, bf16[16,128,128]{2,1,0:T(8,128)(2,1)S(1)}, bf16[512,128]{1,0:T(8,128)(2,1)S(1)}, bf16[512,128]{1,0:...) custom-call(bf16[16,128]{1,0:T(8,128)(2,1)S(1)} %copy-done.4, ...), custom_call_target="tpu_custom_call" | custom-call | bytes 6264832 | tf_op jit(solution)/shard_map/pallas_call | solution.py:389
  10.4 1.9 %collective-permute-done.3.halo = bf16[256,128]{1,0:T(8,128)(2,1)S(1)} collective-permute-done((bf16[256,128]{1,0:T(8,128)(2,1)S(1)}, bf16[256,128]{1,0:T(8,128)(2,1)S(1)}, u32[]{:S(2)}, u32[]{:S(2)}) %collective-permute-start.3) | collective-permute-done | bytes 65568 | tf_op jit(solution)/shard_map/ppermute | solution.py:444
  12.3 1.5 %shard_map.162 = (bf16[256,512]{1,0:T(8,128)(2,1)}, bf16[256,512]{1,0:T(8,128)(2,1)}, bf16[256,512]{1,0:T(8,128)(2,1)S(1)}, bf16[256,640]{1,0:T(8,128)(2,1)S(1)}...) custom-call(bf16[256,128]{1,0:T(8,128)(2,1)S(1)} %collective-permute-done.3.halo, ...), custom_call_target="tpu_custom_call" | custom-call | bytes 4210688 | tf_op jit(solution)/shard_map/pallas_call | solution.py:389
  13.8 8.1 %all_to_all.5.states = f32[8,16,256]{2,1,0:T(8,128)S(1)} all-to-all(f32[8,16,256]{2,1,0:T(8,128)S(1)} %get-tuple-element.70), channel_id=1, replica_groups=mesh['ctx'=8,'ch'=4] {'ctx'}, dimensions={0} | all-to-all | bytes 262144 | tf_op jit(solution)/shard_map/all_to_all | solution.py:499
  21.9 2.3 %shard_map.163 = (bf16[256,512]{1,0:T(8,128)(2,1)S(1)}, bf16[256,512]{1,0:T(8,128)(2,1)S(1)}, bf16[256,512]{1,0:T(8,128)(2,1)}, bf16[256,512]{1,0:T(8,128)(2,1)}...) custom-call(f32[8,16,256]{2,1,0:T(8,128)S(1)} %all_to_all.5.states, f32[4,16,256]{2,1,0:T(8,128)S(1)} %get-tuple-element.71.sub, ...), custom_call_target="tpu_custom_call" | custom-call | bytes 3047424 | tf_op jit(solution)/shard_map/pallas_call | solution.py:389
  24.2 0.0 collective-permute-done.refs_1_
  24.2 0.0 collective-permute-done.2.refs_3_
  24.2 4.9 %collective-permute-done.1.refs_2_ = bf16[256,512]{1,0:T(8,128)(2,1)S(1)} collective-permute-done((bf16[256,512]{1,0:T(8,128)(2,1)}, bf16[256,512]{1,0:T(8,128)(2,1)S(1)}, u32[]{:S(2)}, u32[]{:S(2)}) %collective-permute-start.1) | collective-permute-done | bytes 262176 | tf_op jit(solution)/shard_map/ppermute | solution.py:447
  29.2 2.3 %shard_map.164 = (bf16[256,512]{1,0:T(8,128)(2,1)}, bf16[256,512]{1,0:T(8,128)(2,1)}, f32[4,16,256]{2,1,0:T(8,128)}, bf16[256,128]{1,0:T(8,128)(2,1)}, bf16[40,1...) custom-call(bf16[256,512]{1,0:T(8,128)(2,1)S(1)} %get-tuple-element., ...), custom_call_target="tpu_custom_call" | custom-call | bytes 4341760 | tf_op jit(solution)/shard_map/pallas_call | solution.py:389
  31.5 0.0 collective-permute-start.4
  31.5 1.6 %collective-permute-start.5 = (bf16[40,1024]{1,0:T(8,128)(2,1)}, bf16[40,1024]{1,0:T(8,128)(2,1)S(1)}, u32[]{:S(2)}, u32[]{:S(2)}) collective-permute-start(bf16[40,1024]{1,0:T(8,128)(2,1)} %get-tuple-element.80), channel_id=1, source_target_pairs={{0,8},{4,12},{8,0},{12,4},{16,24},{20,28},{24,16},{28,20},{1,9},{5... | collective-permute-start | bytes 245768 | tf_op jit(solution)/shard_map/ppermute | solution.py:416
  33.0 0.3 collective-permute-start.6
  33.3 1.5 %collective-permute-start.7 = (bf16[40,1024]{1,0:T(8,128)(2,1)}, bf16[40,1024]{1,0:T(8,128)(2,1)S(1)}, u32[]{:S(2)}, u32[]{:S(2)}) collective-permute-start(bf16[40,1024]{1,0:T(8,128)(2,1)} %get-tuple-element.82), channel_id=1, source_target_pairs={{0,16},{4,20},{8,24},{12,28},{16,0},{20,4},{24,8},{28,12},{1,17},{... | collective-permute-start | bytes 245768 | tf_op jit(solution)/shard_map/ppermute | solution.py:416
  34.8 2.0 %shard_map.167 = bf16[256,256]{1,0:T(8,128)(2,1)} custom-call(bf16[256,128]{1,0:T(8,128)(2,1)} %get-tuple-element.98.local, f32[4,16,256]{2,1,0:T(8,128)} %get-tuple-element.86.refs_8_.sub, f32[16,256]{1,0:T(8,128)S(1)} %get-tuple-element.69.rate_t.refs_10_.refs_9_, f32[16,256]{1,0:T(8,128)S(1)} %get-tuple-element.72.coef_t.refs_10_, ...), custom_call_target="tpu_custom_call" | custom-call | bytes 361472 | tf_op jit(solution)/shard_map/pallas_call | solution.py:389
  36.9 1.1 %collective-permute-start.21 = (bf16[256,256]{1,0:T(8,128)(2,1)}, bf16[256,256]{1,0:T(8,128)(2,1)S(1)}, u32[]{:S(2)}, u32[]{:S(2)}) collective-permute-start(bf16[256,256]{1,0:T(8,128)(2,1)} %shard_map.167), channel_id=1, source_target_pairs={{0,28},{4,0},{8,4},{12,8},{16,12},{20,16},{24,20},{28,24},{1,29},{... | collective-permute-start | bytes 393224 | tf_op jit(solution)/shard_map/ppermute | solution.py:553
  38.0 0.0 collective-permute-done.4.refs_1_
  38.0 0.0 collective-permute-start.8
  38.0 0.0 collective-permute-done.5.refs_2_
  38.0 1.9 %collective-permute-start.9 = (bf16[40,1024]{1,0:T(8,128)(2,1)}, bf16[40,1024]{1,0:T(8,128)(2,1)S(1)}, u32[]{:S(2)}, u32[]{:S(2)}) collective-permute-start(bf16[40,1024]{1,0:T(8,128)(2,1)} %get-tuple-element.84), channel_id=1, source_target_pairs={{0,24},{4,28},{8,16},{12,20},{16,8},{20,12},{24,0},{28,4},{1,25},{... | collective-permute-start | bytes 245768 | tf_op jit(solution)/shard_map/ppermute | solution.py:416
  40.0 0.0 collective-permute-done.6.refs_3_
  40.0 0.0 copy-done.8
  40.0 0.0 collective-permute-start.18
  40.0 0.0 collective-permute-done.7.refs_4_
  40.0 0.0 copy-done.9
  40.0 2.0 %collective-permute-start.10 = (bf16[40,1024]{1,0:T(8,128)(2,1)S(1)}, bf16[40,1024]{1,0:T(8,128)(2,1)S(1)}, u32[]{:S(2)}, u32[]{:S(2)}) collective-permute-start(bf16[40,1024]{1,0:T(8,128)(2,1)S(1)} %copy-done.9), channel_id=1, source_target_pairs={{0,28},{4,24},{8,20},{12,16},{16,12},{20,8},{24,4},{28,0},{1,29},{... | collective-permute-start | bytes 245768 | tf_op jit(solution)/shard_map/ppermute | solution.py:416
  42.0 4.4 %collective-permute-done.8.refs_5_ = bf16[40,1024]{1,0:T(8,128)(2,1)S(1)} collective-permute-done((bf16[40,1024]{1,0:T(8,128)(2,1)}, bf16[40,1024]{1,0:T(8,128)(2,1)S(1)}, u32[]{:S(2)}, u32[]{:S(2)}) %collective-permute-start.8) | collective-permute-done | bytes 81952 | tf_op jit(solution)/shard_map/ppermute | solution.py:416
  46.4 0.0 copy-done.7
  46.4 0.0 collective-permute-start.19
  46.4 0.0 collective-permute-done.9.refs_6_
  46.4 0.0 copy-done.6
  46.4 0.1 collective-permute-start.20
  46.5 0.0 collective-permute-done.10.refs_7_
  46.5 4.1 %shard_map.165 = (f32[256,128]{1,0:T(8,128)}, bf16[256,512]{1,0:T(8,128)(2,1)}, bf16[256,512]{1,0:T(8,128)(2,1)}, bf16[40,1024]{1,0:T(8,128)(2,1)}) custom-call(bf16[40,1024]{1,0:T(8,128)(2,1)} %get-tuple-element.78.refs_0_, bf16[40,1024]{1,0:T(8,128)(2,1)S(1)} %collective-permute-done.4.refs_1_, bf16[40,1024]{1,0:T(8,128)(2,1)S(1)} %collective-permute-done.5.refs_2_, ...), custom_call_target="tpu_custom_call" | custom-call | bytes 2606080 | tf_op jit(solution)/shard_map/pallas_call | solution.py:389
  50.6 2.4 %collective-permute-start.16 = (bf16[40,1024]{1,0:T(8,128)(2,1)}, bf16[40,1024]{1,0:T(8,128)(2,1)S(1)}, u32[]{:S(2)}, u32[]{:S(2)}) collective-permute-start(bf16[40,1024]{1,0:T(8,128)(2,1)} %get-tuple-element.89.refs_0_), channel_id=1, source_target_pairs={{0,24},{4,28},{8,16},{12,20},{16,8},{20,12},{24,0},{28,4},{1,25},{... | collective-permute-start | bytes 245768 | tf_op jit(solution)/shard_map/ppermute | solution.py:423
  52.9 0.0 collective-permute-done.21.edge
  52.9 0.7 %collective-permute-start.14 = (bf16[40,1024]{1,0:T(8,128)(2,1)}, bf16[40,1024]{1,0:T(8,128)(2,1)S(1)}, u32[]{:S(2)}, u32[]{:S(2)}) collective-permute-start(bf16[40,1024]{1,0:T(8,128)(2,1)} %get-tuple-element.89.refs_0_), channel_id=1, source_target_pairs={{0,16},{4,20},{8,24},{12,28},{16,0},{20,4},{24,8},{28,12},{1,17},{... | collective-permute-start | bytes 245768 | tf_op jit(solution)/shard_map/ppermute | solution.py:423
  53.6 2.6 %collective-permute-done.16.refs_6_ = bf16[40,1024]{1,0:T(8,128)(2,1)S(1)} collective-permute-done((bf16[40,1024]{1,0:T(8,128)(2,1)}, bf16[40,1024]{1,0:T(8,128)(2,1)S(1)}, u32[]{:S(2)}, u32[]{:S(2)}) %collective-permute-start.16) | collective-permute-done | bytes 81952 | tf_op jit(solution)/shard_map/ppermute | solution.py:423
  56.3 2.2 %collective-permute-start.12 = (bf16[40,1024]{1,0:T(8,128)(2,1)}, bf16[40,1024]{1,0:T(8,128)(2,1)S(1)}, u32[]{:S(2)}, u32[]{:S(2)}) collective-permute-start(bf16[40,1024]{1,0:T(8,128)(2,1)} %get-tuple-element.89.refs_0_), channel_id=1, source_target_pairs={{0,8},{4,12},{8,0},{12,4},{16,24},{20,28},{24,16},{28,20},{1,9},{5... | collective-permute-start | bytes 245768 | tf_op jit(solution)/shard_map/ppermute | solution.py:423
  58.5 0.0 collective-permute-done.14.refs_4_
  58.5 0.0 collective-permute-start.11
  58.5 3.1 %collective-permute-done.12.refs_2_ = bf16[40,1024]{1,0:T(8,128)(2,1)S(1)} collective-permute-done((bf16[40,1024]{1,0:T(8,128)(2,1)}, bf16[40,1024]{1,0:T(8,128)(2,1)S(1)}, u32[]{:S(2)}, u32[]{:S(2)}) %collective-permute-start.12) | collective-permute-done | bytes 81952 | tf_op jit(solution)/shard_map/ppermute | solution.py:423
  61.6 0.0 collective-permute-start.17
  61.6 0.0 collective-permute-done.11.refs_1_
  61.6 0.5 collective-permute-start.15
  62.1 0.0 collective-permute-done.18.refs_9_
  62.1 0.1 collective-permute-start.13
  62.2 3.5 %shard_map.168 = (bf16[256,512]{1,0:T(8,128)(2,1)}, bf16[256,512]{1,0:T(8,128)(2,1)}, bf16[256,512]{1,0:T(8,128)(2,1)}, bf16[256,512]{1,0:T(8,128)(2,1)}, bf16[256,512]{1,0:T(8,128)(2,1)}) custom-call(bf16[256,512]{1,0:T(8,128)(2,1)} %get-tuple-element.95.p2_grad, bf16[256,512]{1,0:T(8,128)(2,1)} %get-tuple-element.96.turned_grad, ...), custom_call_target="tpu_custom_call" | custom-call | bytes 4718592 | tf_op jit(solution)/shard_map/pallas_call | solution.py:389
  65.7 0.0 collective-permute-done.19.refs_10_
  65.7 0.0 collective-permute-done.20.refs_11_
  65.7 0.0 collective-permute-done.17.refs_7_
  65.7 0.0 collective-permute-done.15.refs_5_
  65.7 0.0 collective-permute-done.13.refs_3_
  65.7 1.2 %shard_map.166 = (f32[8,32,1024]{2,1,0:T(8,128)}, f32[16,128]{1,0:T(8,128)}, bf16[256,512]{1,0:T(8,128)(2,1)}) custom-call(bf16[40,1024]{1,0:T(8,128)(2,1)S(1)} %copy-done.3, bf16[40,1024]{1,0:T(8,128)(2,1)S(1)} %collective-permute-done.11.refs_1_, bf16[40,1024]{1,0:T(8,128)(2,1)S(1)} %collective-permute-done.12.refs_2_, ...), custom_call_target="tpu_custom_call" | custom-call | bytes 3022848 | tf_op jit(solution)/shard_map/pallas_call | solution.py:389
  (11 shorter events, 0.0 us)
Async XLA Ops:
  0.6 7.1 %copy-start.2 = (f32[16,16]{1,0:T(8,128)S(1)}, f32[16,16]{1,0:T(8,128)}, u32[]{:S(2)}) copy-start(f32[16,16]{1,0:T(8,128)} %rate_g.1) | copy-start | bytes 3076
  0.6 7.1 %copy-start.5 = (f32[16,16]{1,0:T(8,128)S(1)}, f32[16,16]{1,0:T(8,128)}, u32[]{:S(2)}) copy-start(f32[16,16]{1,0:T(8,128)} %param.18) | copy-start | bytes 3076
  0.7 23.6 %collective-permute-start = (bf16[256,512]{1,0:T(8,128)(2,1)}, bf16[256,512]{1,0:T(8,128)(2,1)S(1)}, u32[]{:S(2)}, u32[]{:S(2)}) collective-permute-start(bf16[256,512]{1,0:T(8,128)(2,1)} %refs_8_.1), channel_id=1, source_target_pairs={{0,1},{1,2},{2,3},{3,0},{4,5},{5,6},{6,7},{7,4},{8,9},{9,10},{10,1... | collective-permute-start | bytes 786440 | tf_op jit(solution)/shard_map/ppermute | solution.py:447
  3.8 20.5 %collective-permute-start.2 = (bf16[256,512]{1,0:T(8,128)(2,1)}, bf16[256,512]{1,0:T(8,128)(2,1)S(1)}, u32[]{:S(2)}, u32[]{:S(2)}) collective-permute-start(bf16[256,512]{1,0:T(8,128)(2,1)} %refs_8_.1), channel_id=1, source_target_pairs={{0,3},{1,0},{2,1},{3,2},{4,7},{5,4},{6,5},{7,6},{8,11},{9,8},{10,9... | collective-permute-start | bytes 786440 | tf_op jit(solution)/shard_map/ppermute | solution.py:447
  5.9 23.3 %collective-permute-start.1 = (bf16[256,512]{1,0:T(8,128)(2,1)}, bf16[256,512]{1,0:T(8,128)(2,1)S(1)}, u32[]{:S(2)}, u32[]{:S(2)}) collective-permute-start(bf16[256,512]{1,0:T(8,128)(2,1)} %refs_8_.1), channel_id=1, source_target_pairs={{0,2},{1,3},{2,0},{3,1},{4,6},{5,7},{6,4},{7,5},{8,10},{9,11},{10,... | collective-permute-start | bytes 786440 | tf_op jit(solution)/shard_map/ppermute | solution.py:447
  7.7 0.7 %copy-start.4 = (bf16[16,128]{1,0:T(8,128)(2,1)S(1)}, bf16[16,128]{1,0:T(8,128)(2,1)}, u32[]{:S(2)}) copy-start(bf16[16,128]{1,0:T(8,128)(2,1)} %refs_0_.1) | copy-start | bytes 12292
  7.7 4.6 %collective-permute-start.3 = (bf16[256,128]{1,0:T(8,128)(2,1)S(1)}, bf16[256,128]{1,0:T(8,128)(2,1)S(1)}, u32[]{:S(2)}, u32[]{:S(2)}) collective-permute-start(bf16[256,128]{1,0:T(8,128)(2,1)S(1)} %multiply_convert_fusion), channel_id=1, source_target_pairs={{0,4},{4,8},{8,12},{12,16},{16,20},{20,24},{24,28},{28,0},{1,5},{5... | collective-permute-start | bytes 196616 | tf_op jit(solution)/shard_map/ppermute | solution.py:444
  29.2 10.8 %copy-start.8 = (bf16[256,512]{1,0:T(8,128)(2,1)S(1)}, bf16[256,512]{1,0:T(8,128)(2,1)}, u32[]{:S(2)}) copy-start(bf16[256,512]{1,0:T(8,128)(2,1)} %get-tuple-element.91) | copy-start | bytes 786436
  29.2 17.2 %copy-start.7 = (bf16[256,512]{1,0:T(8,128)(2,1)S(1)}, bf16[256,512]{1,0:T(8,128)(2,1)}, u32[]{:S(2)}) copy-start(bf16[256,512]{1,0:T(8,128)(2,1)} %get-tuple-element.92) | copy-start | bytes 786436
  29.2 17.3 %copy-start.6 = (bf16[256,512]{1,0:T(8,128)(2,1)S(1)}, bf16[256,512]{1,0:T(8,128)(2,1)}, u32[]{:S(2)}) copy-start(bf16[256,512]{1,0:T(8,128)(2,1)} %get-tuple-element.93) | copy-start | bytes 786436
  31.4 15.1 %copy-start = (bf16[256,512]{1,0:T(8,128)(2,1)S(1)}, bf16[256,512]{1,0:T(8,128)(2,1)}, u32[]{:S(2)}) copy-start(bf16[256,512]{1,0:T(8,128)(2,1)} %get-tuple-element.87.refs_12_) | copy-start | bytes 786436
  31.5 6.6 %collective-permute-start.4 = (bf16[40,1024]{1,0:T(8,128)(2,1)}, bf16[40,1024]{1,0:T(8,128)(2,1)S(1)}, u32[]{:S(2)}, u32[]{:S(2)}) collective-permute-start(bf16[40,1024]{1,0:T(8,128)(2,1)} %get-tuple-element.79), channel_id=1, source_target_pairs={{0,4},{4,0},{8,12},{12,8},{16,20},{20,16},{24,28},{28,24},{1,5},{5... | collective-permute-start | bytes 245768 | tf_op jit(solution)/shard_map/ppermute | solution.py:416
  31.5 6.5 %collective-permute-start.5 = (bf16[40,1024]{1,0:T(8,128)(2,1)}, bf16[40,1024]{1,0:T(8,128)(2,1)S(1)}, u32[]{:S(2)}, u32[]{:S(2)}) collective-permute-start(bf16[40,1024]{1,0:T(8,128)(2,1)} %get-tuple-element.80), channel_id=1, source_target_pairs={{0,8},{4,12},{8,0},{12,4},{16,24},{20,28},{24,16},{28,20},{1,9},{5... | collective-permute-start | bytes 245768 | tf_op jit(solution)/shard_map/ppermute | solution.py:416
  33.0 6.9 %collective-permute-start.6 = (bf16[40,1024]{1,0:T(8,128)(2,1)}, bf16[40,1024]{1,0:T(8,128)(2,1)S(1)}, u32[]{:S(2)}, u32[]{:S(2)}) collective-permute-start(bf16[40,1024]{1,0:T(8,128)(2,1)} %get-tuple-element.81), channel_id=1, source_target_pairs={{0,12},{4,8},{8,4},{12,0},{16,28},{20,24},{24,20},{28,16},{1,13},{... | collective-permute-start | bytes 245768 | tf_op jit(solution)/shard_map/ppermute | solution.py:416
  33.3 6.7 %collective-permute-start.7 = (bf16[40,1024]{1,0:T(8,128)(2,1)}, bf16[40,1024]{1,0:T(8,128)(2,1)S(1)}, u32[]{:S(2)}, u32[]{:S(2)}) collective-permute-start(bf16[40,1024]{1,0:T(8,128)(2,1)} %get-tuple-element.82), channel_id=1, source_target_pairs={{0,16},{4,20},{8,24},{12,28},{16,0},{20,4},{24,8},{28,12},{1,17},{... | collective-permute-start | bytes 245768 | tf_op jit(solution)/shard_map/ppermute | solution.py:416
  34.8 5.2 %copy-start.9 = (bf16[40,1024]{1,0:T(8,128)(2,1)S(1)}, bf16[40,1024]{1,0:T(8,128)(2,1)}, u32[]{:S(2)}) copy-start(bf16[40,1024]{1,0:T(8,128)(2,1)} %get-tuple-element.85) | copy-start | bytes 245764
  36.9 16.0 %collective-permute-start.21 = (bf16[256,256]{1,0:T(8,128)(2,1)}, bf16[256,256]{1,0:T(8,128)(2,1)S(1)}, u32[]{:S(2)}, u32[]{:S(2)}) collective-permute-start(bf16[256,256]{1,0:T(8,128)(2,1)} %shard_map.167), channel_id=1, source_target_pairs={{0,28},{4,0},{8,4},{12,8},{16,12},{20,16},{24,20},{28,24},{1,29},{... | collective-permute-start | bytes 393224 | tf_op jit(solution)/shard_map/ppermute | solution.py:553
  38.0 8.4 %collective-permute-start.8 = (bf16[40,1024]{1,0:T(8,128)(2,1)}, bf16[40,1024]{1,0:T(8,128)(2,1)S(1)}, u32[]{:S(2)}, u32[]{:S(2)}) collective-permute-start(bf16[40,1024]{1,0:T(8,128)(2,1)} %get-tuple-element.83), channel_id=1, source_target_pairs={{0,20},{4,16},{8,28},{12,24},{16,4},{20,0},{24,12},{28,8},{1,21},{... | collective-permute-start | bytes 245768 | tf_op jit(solution)/shard_map/ppermute | solution.py:416
  38.0 8.4 %collective-permute-start.9 = (bf16[40,1024]{1,0:T(8,128)(2,1)}, bf16[40,1024]{1,0:T(8,128)(2,1)S(1)}, u32[]{:S(2)}, u32[]{:S(2)}) collective-permute-start(bf16[40,1024]{1,0:T(8,128)(2,1)} %get-tuple-element.84), channel_id=1, source_target_pairs={{0,24},{4,28},{8,16},{12,20},{16,8},{20,12},{24,0},{28,4},{1,25},{... | collective-permute-start | bytes 245768 | tf_op jit(solution)/shard_map/ppermute | solution.py:416
  40.0 22.1 %collective-permute-start.18 = (bf16[256,512]{1,0:T(8,128)(2,1)S(1)}, bf16[256,512]{1,0:T(8,128)(2,1)S(1)}, u32[]{:S(2)}, u32[]{:S(2)}) collective-permute-start(bf16[256,512]{1,0:T(8,128)(2,1)S(1)} %copy-done.8), channel_id=1, source_target_pairs={{0,1},{1,2},{2,3},{3,0},{4,5},{5,6},{6,7},{7,4},{8,9},{9,10},{10,1... | collective-permute-start | bytes 786440 | tf_op jit(solution)/shard_map/ppermute | solution.py:516
  40.0 6.5 %collective-permute-start.10 = (bf16[40,1024]{1,0:T(8,128)(2,1)S(1)}, bf16[40,1024]{1,0:T(8,128)(2,1)S(1)}, u32[]{:S(2)}, u32[]{:S(2)}) collective-permute-start(bf16[40,1024]{1,0:T(8,128)(2,1)S(1)} %copy-done.9), channel_id=1, source_target_pairs={{0,28},{4,24},{8,20},{12,16},{16,12},{20,8},{24,4},{28,0},{1,29},{... | collective-permute-start | bytes 245768 | tf_op jit(solution)/shard_map/ppermute | solution.py:416
  46.4 19.2 %collective-permute-start.19 = (bf16[256,512]{1,0:T(8,128)(2,1)S(1)}, bf16[256,512]{1,0:T(8,128)(2,1)S(1)}, u32[]{:S(2)}, u32[]{:S(2)}) collective-permute-start(bf16[256,512]{1,0:T(8,128)(2,1)S(1)} %copy-done.7), channel_id=1, source_target_pairs={{0,2},{1,3},{2,0},{3,1},{4,6},{5,7},{6,4},{7,5},{8,10},{9,11},{10,... | collective-permute-start | bytes 786440 | tf_op jit(solution)/shard_map/ppermute | solution.py:516
  46.4 19.2 %collective-permute-start.20 = (bf16[256,512]{1,0:T(8,128)(2,1)S(1)}, bf16[256,512]{1,0:T(8,128)(2,1)S(1)}, u32[]{:S(2)}, u32[]{:S(2)}) collective-permute-start(bf16[256,512]{1,0:T(8,128)(2,1)S(1)} %copy-done.6), channel_id=1, source_target_pairs={{0,3},{1,0},{2,1},{3,2},{4,7},{5,4},{6,5},{7,6},{8,11},{9,8},{10,9... | collective-permute-start | bytes 786440 | tf_op jit(solution)/shard_map/ppermute | solution.py:516
  50.6 5.7 %collective-permute-start.16 = (bf16[40,1024]{1,0:T(8,128)(2,1)}, bf16[40,1024]{1,0:T(8,128)(2,1)S(1)}, u32[]{:S(2)}, u32[]{:S(2)}) collective-permute-start(bf16[40,1024]{1,0:T(8,128)(2,1)} %get-tuple-element.89.refs_0_), channel_id=1, source_target_pairs={{0,24},{4,28},{8,16},{12,20},{16,8},{20,12},{24,0},{28,4},{1,25},{... | collective-permute-start | bytes 245768 | tf_op jit(solution)/shard_map/ppermute | solution.py:423
  52.9 5.5 %collective-permute-start.14 = (bf16[40,1024]{1,0:T(8,128)(2,1)}, bf16[40,1024]{1,0:T(8,128)(2,1)S(1)}, u32[]{:S(2)}, u32[]{:S(2)}) collective-permute-start(bf16[40,1024]{1,0:T(8,128)(2,1)} %get-tuple-element.89.refs_0_), channel_id=1, source_target_pairs={{0,16},{4,20},{8,24},{12,28},{16,0},{20,4},{24,8},{28,12},{1,17},{... | collective-permute-start | bytes 245768 | tf_op jit(solution)/shard_map/ppermute | solution.py:423
  56.3 5.3 %collective-permute-start.12 = (bf16[40,1024]{1,0:T(8,128)(2,1)}, bf16[40,1024]{1,0:T(8,128)(2,1)S(1)}, u32[]{:S(2)}, u32[]{:S(2)}) collective-permute-start(bf16[40,1024]{1,0:T(8,128)(2,1)} %get-tuple-element.89.refs_0_), channel_id=1, source_target_pairs={{0,8},{4,12},{8,0},{12,4},{16,24},{20,28},{24,16},{28,20},{1,9},{5... | collective-permute-start | bytes 245768 | tf_op jit(solution)/shard_map/ppermute | solution.py:423
  58.5 3.1 %collective-permute-start.11 = (bf16[40,1024]{1,0:T(8,128)(2,1)}, bf16[40,1024]{1,0:T(8,128)(2,1)S(1)}, u32[]{:S(2)}, u32[]{:S(2)}) collective-permute-start(bf16[40,1024]{1,0:T(8,128)(2,1)} %get-tuple-element.89.refs_0_), channel_id=1, source_target_pairs={{0,4},{4,0},{8,12},{12,8},{16,20},{20,16},{24,28},{28,24},{1,5},{5... | collective-permute-start | bytes 245768 | tf_op jit(solution)/shard_map/ppermute | solution.py:423
  61.6 4.1 %collective-permute-start.17 = (bf16[40,1024]{1,0:T(8,128)(2,1)S(1)}, bf16[40,1024]{1,0:T(8,128)(2,1)S(1)}, u32[]{:S(2)}, u32[]{:S(2)}) collective-permute-start(bf16[40,1024]{1,0:T(8,128)(2,1)S(1)} %collective-permute-done.16.refs_6_), channel_id=1, source_target_pairs={{0,4},{4,0},{8,12},{12,8},{16,20},{20,16},{24,28},{28,24},{1,5},{5... | collective-permute-start | bytes 245768 | tf_op jit(solution)/shard_map/ppermute | solution.py:425
  61.6 4.1 %collective-permute-start.15 = (bf16[40,1024]{1,0:T(8,128)(2,1)S(1)}, bf16[40,1024]{1,0:T(8,128)(2,1)S(1)}, u32[]{:S(2)}, u32[]{:S(2)}) collective-permute-start(bf16[40,1024]{1,0:T(8,128)(2,1)S(1)} %collective-permute-done.14.refs_4_), channel_id=1, source_target_pairs={{0,4},{4,0},{8,12},{12,8},{16,20},{20,16},{24,28},{28,24},{1,5},{5... | collective-permute-start | bytes 245768 | tf_op jit(solution)/shard_map/ppermute | solution.py:425
  62.1 3.6 %collective-permute-start.13 = (bf16[40,1024]{1,0:T(8,128)(2,1)S(1)}, bf16[40,1024]{1,0:T(8,128)(2,1)S(1)}, u32[]{:S(2)}, u32[]{:S(2)}) collective-permute-start(bf16[40,1024]{1,0:T(8,128)(2,1)S(1)} %collective-permute-done.12.refs_2_), channel_id=1, source_target_pairs={{0,4},{4,0},{8,12},{12,8},{16,20},{20,16},{24,28},{28,24},{1,5},{5... | collective-permute-start | bytes 245768 | tf_op jit(solution)/shard_map/ppermute | solution.py:425
  62.2 3.5 %copy-start.1 = (bf16[256,512]{1,0:T(8,128)(2,1)S(1)}, bf16[256,512]{1,0:T(8,128)(2,1)}, u32[]{:S(2)}) copy-start(bf16[256,512]{1,0:T(8,128)(2,1)} %get-tuple-element.90.refs_8_) | copy-start | bytes 786436
  62.2 3.5 %copy-start.3 = (bf16[40,1024]{1,0:T(8,128)(2,1)S(1)}, bf16[40,1024]{1,0:T(8,128)(2,1)}, u32[]{:S(2)}) copy-start(bf16[40,1024]{1,0:T(8,128)(2,1)} %get-tuple-element.89.refs_0_) | copy-start | bytes 245764

commit v2 on v1

--- a/solution.py
+++ b/solution.py
@@ -98,14 +98,14 @@
     for i, part in enumerate(split(value)):
         for j in range(2):
             at = (2 * i + j) * chans
-            ref[first:, at : at + chans] = part[j * half : (j + 1) * half]
+            ref[first : first + half, at : at + chans] = part[j * half : (j + 1) * half]
     width = ref.shape[1]
     if 4 * chans < width:
-        ref[first:, 4 * chans :] = jnp.zeros((half, width - 4 * chans), BF16)
-
-
-def unpack_rows(ref, first, chans):
-    parts = [ref[first:, i * chans : (i + 1) * chans].astype(F32) for i in range(4)]
+        ref[first : first + half, 4 * chans :] = jnp.zeros((half, width - 4 * chans), BF16)
+
+
+def unpack_rows(ref, first, half, chans):
+    parts = [ref[first : first + half, i * chans : (i + 1) * chans].astype(F32) for i in range(4)]
     return jnp.concatenate([parts[0] + parts[2], parts[1] + parts[3]], axis=0)
 
 
@@ -270,13 +270,26 @@
     if fused:
         rows = chans // n_ctx
         me = lax.axis_index("ctx")
-        for k in range(n_ctx):
-            at = pl.multiple_of(jnp.bitwise_xor(me, k) * rows, rows)
-            sent[k][0:rows] = whole[pl.ds(at, rows), :]
-            pack_rows(sent[k], rows, total)
+        for i in range(n_ctx // 2):
+            for j in range(2):
+                at = pl.multiple_of(jnp.bitwise_xor(me, 2 * i + j) * rows, rows)
+                sent[j][i * rows : (i + 1) * rows] = whole[pl.ds(at, rows), :]
+        pack_rows(sent[1], n_ctx // 2 * rows, total)
+        pack_rows(sent[2], 0, total)
     else:
         for d in range(n_ctx):
             sent[0][d] = total
+
+
+def pair_kernel(size, kept, own, got, local, sub, rate_t, coef_t, rate_g, ahead, edge, *out):
+    half = own.shape[0]
+    rows = kept.shape[0] // len(out)
+    for i, block in enumerate(out):
+        at = slice(i * rows, (i + 1) * rows)
+        block[0:rows] = (kept[at].astype(F32) + got[at].astype(F32)).astype(BF16)
+        block[rows : rows + half] = own[...]
+        block[rows + half :] = got[len(out) * rows :]
+    between_kernel(size, local, sub, rate_t, coef_t, rate_g, ahead, edge)
 
 
 def between_kernel(size, local, sub, rate_t, coef_t, rate_g, ahead, edge):
@@ -293,7 +306,7 @@
 
 
 def fourth_kernel(size, fused, n_ctx, *refs):
-    moved = refs[: n_ctx if fused else 1]
+    moved = refs[: n_ctx // 2 if fused else 1]
     (sub, rate_t, coef_t, rate_g, local, q1, k2, mirrored) = refs[len(moved) : len(moved) + 8]
     (beside, p2_grad, turned_grad, out) = refs[len(moved) + 8 :]
     modes, chans = rate_t.shape
@@ -307,7 +320,11 @@
     beyond = jnp.zeros(rate.shape, F32)
     following = jnp.zeros(rate.shape, F32)
     for k in range(n_ctx):
-        state = unpack_rows(moved[k], rows, chans) if fused else moved[0][k]
+        if fused:
+            at = rows + k % 2 * (modes // 2)
+            state = unpack_rows(moved[k // 2], at, modes // 2, chans)
+        else:
+            state = moved[0][k]
         gap = (jnp.bitwise_xor(me, k) if fused else k) - me - 2
         factor = jnp.exp(-rate * (length * jnp.maximum(gap, 0).astype(F32)))
         beyond = beyond + jnp.where(gap >= 0, factor * state, 0.0)
@@ -338,8 +355,8 @@
     filter_rows = jnp.concatenate(filters, axis=0)
     if fused:
         total = moved[0][0:rows].astype(F32)
-        for k in range(1, n_ctx):
-            total = total + moved[k][0:rows].astype(F32)
+        for block in moved[1:]:
+            total = total + block[0:rows].astype(F32)
         out[0:rows] = total.astype(BF16)
         pack_rows(out, rows, filter_rows)
     else:
@@ -373,7 +390,7 @@
     total = None
     for k in range(n_ctx):
         weight_out[jnp.bitwise_xor(me, k)] = scale * moved[k][0:rows].astype(F32)
-        term = unpack_rows(moved[k], rows, BLK)
+        term = unpack_rows(moved[k], rows, moved[k].shape[0] - rows, BLK)
         total = term if total is None else total + term
     filter_out[...] = scale * total
     summed = parts[0][...].astype(F32)
@@ -412,8 +429,8 @@
 
 def exchange(blocks, count):
     out = [blocks[0]]
-    for k in range(1, count):
-        out.append(lax.ppermute(blocks[k], "ctx", [(i, i ^ k) for i in range(count)]))
+    for i in range(1, count // 2):
+        out.append(lax.ppermute(blocks[i], "ctx", [(d, d ^ (2 * i)) for d in range(count)]))
     return out
 
 
@@ -516,7 +533,11 @@
         mixed_parts.append(lax.ppermute(parts[k], "ch", around(n_ch, k)))
     packed = ((rows + modes // 2, out_chans), BF16)
     if fused:
-        sent_shapes = [packed] * n_ctx
+        sent_shapes = [
+            ((chans // 2, out_chans), BF16),
+            ((chans // 2 + modes // 2, out_chans), BF16),
+            ((modes // 2, out_chans), BF16),
+        ]
     else:
         sent_shapes = [((n_ctx, modes, chans), F32), ((chans, out_chans), F32)]
     q2_grad, local_back, sub_back, first_back, *sent_back = call(
@@ -534,22 +555,31 @@
         scratch=[pltpu.VMEM((chans, out_chans), BF16), pltpu.VMEM((chans, length), BF16)],
         name="third",
     )
+    edge_args = (first_back, sub_back, rate_t, coef_t, rate, ahead)
+    edge_shape = ((chans, 2 * BLK), BF16)
     if fused:
-        states_back = exchange(sent_back, n_ctx)
+        kept, crossing, own = sent_back
+        got = lax.ppermute(crossing, "ctx", [(i, i ^ 1) for i in range(n_ctx)])
+        edge, *blocks_back = call(
+            functools.partial(pair_kernel, size),
+            [edge_shape] + [((rows + modes, out_chans), BF16)] * (n_ctx // 2),
+            kept,
+            own,
+            got,
+            *edge_args,
+            far=(0, 1, 3, 4, 8),
+            name="pair",
+        )
+        states_back = exchange(blocks_back, n_ctx)
     else:
         states_back = [lax.all_to_all(sent_back[0], "ctx", 0, 0, tiled=True)]
-    (edge,) = call(
-        functools.partial(between_kernel, size),
-        [((chans, 2 * BLK), BF16)],
-        first_back,
-        sub_back,
-        rate_t,
-        coef_t,
-        rate,
-        ahead,
-        far=(0, 1, 5),
-        name="between",
-    )
+        (edge,) = call(
+            functools.partial(between_kernel, size),
+            [edge_shape],
+            *edge_args,
+            far=(0, 1, 5),
+            name="between",
+        )
     next_edge = lax.ppermute(edge, "ctx", around(n_ctx, -1))
     beside, p2_grad, turned_grad, last = call(
         functools.partial(fourth_kernel, size, fused, n_ctx),
@@ -563,7 +593,7 @@
         late_q1,
         late_k2,
         mirrored,
-        far=(0, n_ctx) if fused else (),
+        far=(0, n_ctx // 2) if fused else (),
         name="fourth",
     )
     scale = 1.0 / math.sqrt(length * n_ctx)

time: 67.3 us -> 62.9 us (0.935)
  waiting for transfers between devices: 17 us -> 14.5 us
  starting transfers between devices: 20.6 us -> 18.4 us
    ppermute x3, starting transfers between devices: 0.06 us -> 4.13 us  [on_device(): mixed_parts.append(lax.ppermute(parts[k], 'ch', around(n_ch, k)))]
    ppermute x7 -> x4, starting transfers between devices: 7.34 us -> 3.5 us  [the longest x3 3.49 us: exchange(): lax.ppermute(blocks[i], 'ctx', [(d, d ^ 2 * i) for d in range(count)])]
    ppermute x4, waiting for transfers between devices: 5.72 us -> 2.64 us  [gather(): out[k] = lax.ppermute(block, 'ctx', [(i, i ^ k) for i in range(count)])]
    ppermute x3, waiting for transfers between devices: 0.01 us -> 2.26 us  [on_device(): mixed_parts.append(lax.ppermute(parts[k], 'ch', around(n_ch, k)))]
    ppermute x4, starting transfers between devices: 5.28 us -> 3.61 us  [gather(): out[k] = lax.ppermute(block, 'ctx', [(i, i ^ k) for i in range(count)])]
    ppermute x7 -> x4, waiting for transfers between devices: 4.41 us -> 2.82 us  [the longest x3 2.82 us: exchange(): lax.ppermute(blocks[i], 'ctx', [(d, d ^ 2 * i) for d in range(count)])]
  transfers between devices with their start and end apart: 22 -> 19, of which waited for: 5 -> 8; matrix products, arithmetic and copies ran while one was open for 1% -> 1% of each run, Pallas kernels for 23% -> 25%
where the time goes in v2:
time: 62.9 us; the launch traced here: 62.3 us
  Pallas kernels  18.9 us (30%)
  starting transfers between devices  18.4 us (29%)
  waiting for transfers between devices  14.5 us (23%)
  blocking collectives  8.11 us (13%)
  other arithmetic  0.91 us (1%)
  between operations  0.78 us (1%)
    pallas_call x8, Pallas kernels, call(): pl.pallas_call(kernel, out_shape=[pltpu.VMEM(s, t) if i in held else pltp...  18.9 us
    all_to_all x1, blocking collectives, on_device(): states = lax.all_to_all(sent, 'ctx', 0, 0, tiled=True)  8.11 us
    ppermute x3, starting transfers between devices, on_device(): grads.append(lax.ppermute(out_grad, 'ch', around(n_ch, k)))  6.14 us
    ppermute x3, waiting for transfers between devices, on_device(): grads.append(lax.ppermute(out_grad, 'ch', around(n_ch, k)))  4.9 us
    ppermute x3, starting transfers between devices, on_device(): mixed_parts.append(lax.ppermute(parts[k], 'ch', around(n_ch, k)))  4.13 us
    ppermute x4, starting transfers between devices, gather(): out[k] = lax.ppermute(block, 'ctx', [(i, i ^ k) for i in range(count)])  3.61 us
    ppermute x3, starting transfers between devices, exchange(): lax.ppermute(blocks[i], 'ctx', [(d, d ^ 2 * i) for d in range(count)])  3.49 us
    ppermute x3, waiting for transfers between devices, exchange(): lax.ppermute(blocks[i], 'ctx', [(d, d ^ 2 * i) for d in range(count)])  2.82 us
  transfers between devices with their start and end apart: 19, of which 8 were waited for; matrix products, arithmetic and copies ran while one was open for 1% of the time, Pallas kernels for 25%

profile of v2, /device:TPU:0, one launch (start us, length us, event | category | flops | bytes accessed | tf_op | source)
XLA Modules:
  0.0 62.3 jit_solution(1855993305490043889)
XLA Ops:
  0.6 0.0 copy-start.2
  0.6 0.0 copy-start.5
  0.7 3.1 %collective-permute-start = (bf16[256,512]{1,0:T(8,128)(2,1)}, bf16[256,512]{1,0:T(8,128)(2,1)S(1)}, u32[]{:S(2)}, u32[]{:S(2)}) collective-permute-start(bf16[256,512]{1,0:T(8,128)(2,1)} %refs_8_.1), channel_id=1, source_target_pairs={{0,1},{1,2},{2,3},{3,0},{4,5},{5,6},{6,7},{7,4},{8,9},{9,10},{10,1... | collective-permute-start | bytes 786440 | tf_op jit(solution)/shard_map/ppermute | solution.py:464
  3.8 2.1 %collective-permute-start.2 = (bf16[256,512]{1,0:T(8,128)(2,1)}, bf16[256,512]{1,0:T(8,128)(2,1)S(1)}, u32[]{:S(2)}, u32[]{:S(2)}) collective-permute-start(bf16[256,512]{1,0:T(8,128)(2,1)} %refs_8_.1), channel_id=1, source_target_pairs={{0,3},{1,0},{2,1},{3,2},{4,7},{5,4},{6,5},{7,6},{8,11},{9,8},{10,9... | collective-permute-start | bytes 786440 | tf_op jit(solution)/shard_map/ppermute | solution.py:464
  5.9 0.9 %collective-permute-start.1 = (bf16[256,512]{1,0:T(8,128)(2,1)}, bf16[256,512]{1,0:T(8,128)(2,1)S(1)}, u32[]{:S(2)}, u32[]{:S(2)}) collective-permute-start(bf16[256,512]{1,0:T(8,128)(2,1)} %refs_8_.1), channel_id=1, source_target_pairs={{0,2},{1,3},{2,0},{3,1},{4,6},{5,7},{6,4},{7,5},{8,10},{9,11},{10,... | collective-permute-start | bytes 786440 | tf_op jit(solution)/shard_map/ppermute | solution.py:464
  6.8 0.9 %multiply_convert_fusion = bf16[256,128]{1,0:T(8,128)(2,1)S(1)} fusion(bf16[256,512]{1,0:T(8,128)(2,1)} %v1.1, bf16[256,512]{1,0:T(8,128)(2,1)} %k1.1), kind=kLoop, calls=%fused_computation | loop fusion | flops 131072 | bytes 196608 | tf_op jit(solution)/shard_map/convert_element_type | solution.py:460
  7.7 0.0 copy-start.4
  7.7 0.1 collective-permute-start.3
  7.8 0.0 copy-done.2
  7.8 0.0 copy-done.5
  7.8 0.6 copy-done.4
  8.4 2.0 %shard_map.161 = (bf16[16,256,128]{2,1,0:T(8,128)(2,1)S(1)}, bf16[16,128,128]{2,1,0:T(8,128)(2,1)S(1)}, bf16[512,128]{1,0:T(8,128)(2,1)S(1)}, bf16[512,128]{1,0:...) custom-call(bf16[16,128]{1,0:T(8,128)(2,1)S(1)} %copy-done.4, ...), custom_call_target="tpu_custom_call" | custom-call | bytes 6264832 | tf_op jit(solution)/shard_map/pallas_call | solution.py:406
  10.4 1.9 %collective-permute-done.3.halo = bf16[256,128]{1,0:T(8,128)(2,1)S(1)} collective-permute-done((bf16[256,128]{1,0:T(8,128)(2,1)S(1)}, bf16[256,128]{1,0:T(8,128)(2,1)S(1)}, u32[]{:S(2)}, u32[]{:S(2)}) %collective-permute-start.3) | collective-permute-done | bytes 65568 | tf_op jit(solution)/shard_map/ppermute | solution.py:461
  12.3 1.5 %shard_map.162 = (bf16[256,512]{1,0:T(8,128)(2,1)}, bf16[256,512]{1,0:T(8,128)(2,1)}, bf16[256,512]{1,0:T(8,128)(2,1)S(1)}, bf16[256,640]{1,0:T(8,128)(2,1)S(1)}...) custom-call(bf16[256,128]{1,0:T(8,128)(2,1)S(1)} %collective-permute-done.3.halo, ...), custom_call_target="tpu_custom_call" | custom-call | bytes 4210688 | tf_op jit(solution)/shard_map/pallas_call | solution.py:406
  13.8 8.1 %all_to_all.5.states = f32[8,16,256]{2,1,0:T(8,128)S(1)} all-to-all(f32[8,16,256]{2,1,0:T(8,128)S(1)} %get-tuple-element.70), channel_id=1, replica_groups=mesh['ctx'=8,'ch'=4] {'ctx'}, dimensions={0} | all-to-all | bytes 262144 | tf_op jit(solution)/shard_map/all_to_all | solution.py:516
  22.0 2.3 %shard_map.163 = (bf16[256,512]{1,0:T(8,128)(2,1)S(1)}, bf16[256,512]{1,0:T(8,128)(2,1)S(1)}, bf16[256,512]{1,0:T(8,128)(2,1)}, bf16[256,512]{1,0:T(8,128)(2,1)}...) custom-call(f32[8,16,256]{2,1,0:T(8,128)S(1)} %all_to_all.5.states, f32[4,16,256]{2,1,0:T(8,128)S(1)} %get-tuple-element.71.sub, ...), custom_call_target="tpu_custom_call" | custom-call | bytes 3047424 | tf_op jit(solution)/shard_map/pallas_call | solution.py:406
  24.3 0.0 collective-permute-done.refs_1_
  24.3 0.0 collective-permute-done.2.refs_3_
  24.3 4.9 %collective-permute-done.1.refs_2_ = bf16[256,512]{1,0:T(8,128)(2,1)S(1)} collective-permute-done((bf16[256,512]{1,0:T(8,128)(2,1)}, bf16[256,512]{1,0:T(8,128)(2,1)S(1)}, u32[]{:S(2)}, u32[]{:S(2)}) %collective-permute-start.1) | collective-permute-done | bytes 262176 | tf_op jit(solution)/shard_map/ppermute | solution.py:464
  29.2 0.0 copy-start.8
  29.2 0.0 copy-start.7
  29.2 2.3 %shard_map.164 = (bf16[256,512]{1,0:T(8,128)(2,1)}, bf16[256,512]{1,0:T(8,128)(2,1)}, f32[4,16,256]{2,1,0:T(8,128)}, bf16[256,128]{1,0:T(8,128)(2,1)}, bf16[128,...) custom-call(bf16[256,512]{1,0:T(8,128)(2,1)S(1)} %get-tuple-element.59.refs_0_, ...), custom_call_target="tpu_custom_call" | custom-call | bytes 4243456 | tf_op jit(solution)/shard_map/pallas_call | solution.py:406
  31.4 0.0 collective-permute-start.4
  31.4 0.0 copy-done.8
  31.4 0.0 collective-permute-start.15
  31.5 0.0 copy-done.7
  31.5 2.2 %collective-permute-start.16 = (bf16[256,512]{1,0:T(8,128)(2,1)S(1)}, bf16[256,512]{1,0:T(8,128)(2,1)S(1)}, u32[]{:S(2)}, u32[]{:S(2)}) collective-permute-start(bf16[256,512]{1,0:T(8,128)(2,1)S(1)} %copy-done.7), channel_id=1, source_target_pairs={{0,2},{1,3},{2,0},{3,1},{4,6},{5,7},{6,4},{7,5},{8,10},{9,11},{10,... | collective-permute-start | bytes 786440 | tf_op jit(solution)/shard_map/ppermute | solution.py:533
  33.6 0.0 collective-permute-done.4.got
  33.7 0.0 copy-start.6
  33.7 0.0 copy-start
  33.7 2.3 %shard_map.165 = (bf16[256,256]{1,0:T(8,128)(2,1)}, bf16[48,1024]{1,0:T(8,128)(2,1)}, bf16[48,1024]{1,0:T(8,128)(2,1)}, bf16[48,1024]{1,0:T(8,128)(2,1)}, bf16[48,1024]{1,0:T(8,128)(2,1)}) custom-call(bf16[128,1024]{1,0:T(8,128)(2,1)} %get-tuple-element.78.kept, bf16[8,1024]{1,0:T(8,128)(2,1)} %get-tuple-element.79.own, ...), custom_call_target="tpu_custom_call" | custom-call | bytes 1311744 | tf_op jit(solution)/shard_map/pallas_call | solution.py:406
  35.9 1.5 %collective-permute-start.5 = (bf16[48,1024]{1,0:T(8,128)(2,1)}, bf16[48,1024]{1,0:T(8,128)(2,1)S(1)}, u32[]{:S(2)}, u32[]{:S(2)}) collective-permute-start(bf16[48,1024]{1,0:T(8,128)(2,1)} %get-tuple-element.85), channel_id=1, source_target_pairs={{0,8},{4,12},{8,0},{12,4},{16,24},{20,28},{24,16},{28,20},{1,9},{5... | collective-permute-start | bytes 294920 | tf_op jit(solution)/shard_map/ppermute | solution.py:433
  37.4 1.5 %collective-permute-start.6 = (bf16[48,1024]{1,0:T(8,128)(2,1)}, bf16[48,1024]{1,0:T(8,128)(2,1)S(1)}, u32[]{:S(2)}, u32[]{:S(2)}) collective-permute-start(bf16[48,1024]{1,0:T(8,128)(2,1)} %get-tuple-element.86), channel_id=1, source_target_pairs={{0,16},{4,20},{8,24},{12,28},{16,0},{20,4},{24,8},{28,12},{1,17},{... | collective-permute-start | bytes 294920 | tf_op jit(solution)/shard_map/ppermute | solution.py:433
  38.9 0.5 collective-permute-start.7
  39.4 1.3 %collective-permute-done.5.refs_1_ = bf16[48,1024]{1,0:T(8,128)(2,1)S(1)} collective-permute-done((bf16[48,1024]{1,0:T(8,128)(2,1)}, bf16[48,1024]{1,0:T(8,128)(2,1)S(1)}, u32[]{:S(2)}, u32[]{:S(2)}) %collective-permute-start.5) | collective-permute-done | bytes 98336 | tf_op jit(solution)/shard_map/ppermute | solution.py:433
  40.7 0.0 copy-done.6
  40.7 1.9 %collective-permute-start.17 = (bf16[256,512]{1,0:T(8,128)(2,1)S(1)}, bf16[256,512]{1,0:T(8,128)(2,1)S(1)}, u32[]{:S(2)}, u32[]{:S(2)}) collective-permute-start(bf16[256,512]{1,0:T(8,128)(2,1)S(1)} %copy-done.6), channel_id=1, source_target_pairs={{0,3},{1,0},{2,1},{3,2},{4,7},{5,4},{6,5},{7,6},{8,11},{9,8},{10,9... | collective-permute-start | bytes 786440 | tf_op jit(solution)/shard_map/ppermute | solution.py:533
  42.7 0.6 %collective-permute-done.6.refs_2_ = bf16[48,1024]{1,0:T(8,128)(2,1)S(1)} collective-permute-done((bf16[48,1024]{1,0:T(8,128)(2,1)}, bf16[48,1024]{1,0:T(8,128)(2,1)S(1)}, u32[]{:S(2)}, u32[]{:S(2)}) %collective-permute-start.6) | collective-permute-done | bytes 98336 | tf_op jit(solution)/shard_map/ppermute | solution.py:433
  43.3 0.5 collective-permute-start.18
  43.8 0.8 %collective-permute-done.7.refs_3_ = bf16[48,1024]{1,0:T(8,128)(2,1)S(1)} collective-permute-done((bf16[48,1024]{1,0:T(8,128)(2,1)}, bf16[48,1024]{1,0:T(8,128)(2,1)S(1)}, u32[]{:S(2)}, u32[]{:S(2)}) %collective-permute-start.7) | collective-permute-done | bytes 98336 | tf_op jit(solution)/shard_map/ppermute | solution.py:433
  44.6 0.0 copy-done
  44.7 3.9 %shard_map.166 = (f32[256,128]{1,0:T(8,128)}, bf16[256,512]{1,0:T(8,128)(2,1)}, bf16[256,512]{1,0:T(8,128)(2,1)}, bf16[40,1024]{1,0:T(8,128)(2,1)}) custom-call(bf16[48,1024]{1,0:T(8,128)(2,1)} %get-tuple-element.84.refs_0_, bf16[48,1024]{1,0:T(8,128)(2,1)S(1)} %collective-permute-done.5.refs_1_, bf16[48,1024]{1,0:T(8,128)(2,1)S(1)} %collective-permute-done.6.refs_2_, ...), custom_call_target="tpu_custom_call" | custom-call | bytes 2343936 | tf_op jit(solution)/shard_map/pallas_call | solution.py:406
  48.5 1.2 %collective-permute-start.13 = (bf16[40,1024]{1,0:T(8,128)(2,1)}, bf16[40,1024]{1,0:T(8,128)(2,1)S(1)}, u32[]{:S(2)}, u32[]{:S(2)}) collective-permute-start(bf16[40,1024]{1,0:T(8,128)(2,1)} %get-tuple-element.90.refs_0_), channel_id=1, source_target_pairs={{0,24},{4,28},{8,16},{12,20},{16,8},{20,12},{24,0},{28,4},{1,25},{... | collective-permute-start | bytes 245768 | tf_op jit(solution)/shard_map/ppermute | solution.py:440
  49.7 0.0 collective-permute-done.15.refs_9_
  49.7 0.9 %collective-permute-start.11 = (bf16[40,1024]{1,0:T(8,128)(2,1)}, bf16[40,1024]{1,0:T(8,128)(2,1)S(1)}, u32[]{:S(2)}, u32[]{:S(2)}) collective-permute-start(bf16[40,1024]{1,0:T(8,128)(2,1)} %get-tuple-element.90.refs_0_), channel_id=1, source_target_pairs={{0,16},{4,20},{8,24},{12,28},{16,0},{20,4},{24,8},{28,12},{1,17},{... | collective-permute-start | bytes 245768 | tf_op jit(solution)/shard_map/ppermute | solution.py:440
  50.6 2.3 %collective-permute-done.16.refs_10_ = bf16[256,512]{1,0:T(8,128)(2,1)S(1)} collective-permute-done((bf16[256,512]{1,0:T(8,128)(2,1)S(1)}, bf16[256,512]{1,0:T(8,128)(2,1)S(1)}, u32[]{:S(2)}, u32[]{:S(2)}) %collective-permute-start.16) | collective-permute-done | bytes 262176 | tf_op jit(solution)/shard_map/ppermute | solution.py:533
  52.9 1.5 %collective-permute-start.9 = (bf16[40,1024]{1,0:T(8,128)(2,1)}, bf16[40,1024]{1,0:T(8,128)(2,1)S(1)}, u32[]{:S(2)}, u32[]{:S(2)}) collective-permute-start(bf16[40,1024]{1,0:T(8,128)(2,1)} %get-tuple-element.90.refs_0_), channel_id=1, source_target_pairs={{0,8},{4,12},{8,0},{12,4},{16,24},{20,28},{24,16},{28,20},{1,9},{5... | collective-permute-start | bytes 245768 | tf_op jit(solution)/shard_map/ppermute | solution.py:440
  54.4 0.0 collective-permute-done.18.edge
  54.4 0.0 collective-permute-start.8
  54.4 0.0 collective-permute-done.13.refs_6_
  54.4 0.5 collective-permute-start.14
  54.9 0.4 collective-permute-done.11.refs_4_
  55.4 0.0 collective-permute-start.12
  55.4 2.2 %collective-permute-done.9.refs_2_ = bf16[40,1024]{1,0:T(8,128)(2,1)S(1)} collective-permute-done((bf16[40,1024]{1,0:T(8,128)(2,1)}, bf16[40,1024]{1,0:T(8,128)(2,1)S(1)}, u32[]{:S(2)}, u32[]{:S(2)}) %collective-permute-start.9) | collective-permute-done | bytes 81952 | tf_op jit(solution)/shard_map/ppermute | solution.py:440
  57.6 0.0 collective-permute-start.10
  57.6 3.5 %shard_map.168 = (bf16[256,512]{1,0:T(8,128)(2,1)}, bf16[256,512]{1,0:T(8,128)(2,1)}, bf16[256,512]{1,0:T(8,128)(2,1)}, bf16[256,512]{1,0:T(8,128)(2,1)}, bf16[256,512]{1,0:T(8,128)(2,1)}) custom-call(bf16[256,512]{1,0:T(8,128)(2,1)} %get-tuple-element.96.p2_grad, bf16[256,512]{1,0:T(8,128)(2,1)} %get-tuple-element.97.turned_grad, ...), custom_call_target="tpu_custom_call" | custom-call | bytes 4718592 | tf_op jit(solution)/shard_map/pallas_call | solution.py:406
  61.1 0.0 collective-permute-done.17.refs_11_
  61.1 0.0 collective-permute-done.8.refs_1_
  61.1 0.0 collective-permute-done.14.refs_7_
  61.1 0.0 collective-permute-done.12.refs_5_
  61.1 0.0 collective-permute-done.10.refs_3_
  61.1 0.0 copy-done.1
  61.1 0.0 copy-done.3
  61.1 1.2 %shard_map.167 = (f32[8,32,1024]{2,1,0:T(8,128)}, f32[16,128]{1,0:T(8,128)}, bf16[256,512]{1,0:T(8,128)(2,1)}) custom-call(bf16[40,1024]{1,0:T(8,128)(2,1)S(1)} %copy-done.3, bf16[40,1024]{1,0:T(8,128)(2,1)S(1)} %collective-permute-done.8.refs_1_, bf16[40,1024]{1,0:T(8,128)(2,1)S(1)} %collective-permute-done.9.refs_2_, ...), custom_call_target="tpu_custom_call" | custom-call | bytes 3022848 | tf_op jit(solution)/shard_map/pallas_call | solution.py:406
  (3 shorter events, 0.0 us)
Async XLA Ops:
  0.6 7.1 %copy-start.2 = (f32[16,16]{1,0:T(8,128)S(1)}, f32[16,16]{1,0:T(8,128)}, u32[]{:S(2)}) copy-start(f32[16,16]{1,0:T(8,128)} %refs_7_.3) | copy-start | bytes 3076
  0.6 7.1 %copy-start.5 = (f32[16,16]{1,0:T(8,128)S(1)}, f32[16,16]{1,0:T(8,128)}, u32[]{:S(2)}) copy-start(f32[16,16]{1,0:T(8,128)} %param.18) | copy-start | bytes 3076
  0.7 23.6 %collective-permute-start = (bf16[256,512]{1,0:T(8,128)(2,1)}, bf16[256,512]{1,0:T(8,128)(2,1)S(1)}, u32[]{:S(2)}, u32[]{:S(2)}) collective-permute-start(bf16[256,512]{1,0:T(8,128)(2,1)} %refs_8_.1), channel_id=1, source_target_pairs={{0,1},{1,2},{2,3},{3,0},{4,5},{5,6},{6,7},{7,4},{8,9},{9,10},{10,1... | collective-permute-start | bytes 786440 | tf_op jit(solution)/shard_map/ppermute | solution.py:464
  3.8 20.5 %collective-permute-start.2 = (bf16[256,512]{1,0:T(8,128)(2,1)}, bf16[256,512]{1,0:T(8,128)(2,1)S(1)}, u32[]{:S(2)}, u32[]{:S(2)}) collective-permute-start(bf16[256,512]{1,0:T(8,128)(2,1)} %refs_8_.1), channel_id=1, source_target_pairs={{0,3},{1,0},{2,1},{3,2},{4,7},{5,4},{6,5},{7,6},{8,11},{9,8},{10,9... | collective-permute-start | bytes 786440 | tf_op jit(solution)/shard_map/ppermute | solution.py:464
  5.9 23.3 %collective-permute-start.1 = (bf16[256,512]{1,0:T(8,128)(2,1)}, bf16[256,512]{1,0:T(8,128)(2,1)S(1)}, u32[]{:S(2)}, u32[]{:S(2)}) collective-permute-start(bf16[256,512]{1,0:T(8,128)(2,1)} %refs_8_.1), channel_id=1, source_target_pairs={{0,2},{1,3},{2,0},{3,1},{4,6},{5,7},{6,4},{7,5},{8,10},{9,11},{10,... | collective-permute-start | bytes 786440 | tf_op jit(solution)/shard_map/ppermute | solution.py:464
  7.7 0.7 %copy-start.4 = (bf16[16,128]{1,0:T(8,128)(2,1)S(1)}, bf16[16,128]{1,0:T(8,128)(2,1)}, u32[]{:S(2)}) copy-start(bf16[16,128]{1,0:T(8,128)(2,1)} %refs_0_.1) | copy-start | bytes 12292
  7.7 4.6 %collective-permute-start.3 = (bf16[256,128]{1,0:T(8,128)(2,1)S(1)}, bf16[256,128]{1,0:T(8,128)(2,1)S(1)}, u32[]{:S(2)}, u32[]{:S(2)}) collective-permute-start(bf16[256,128]{1,0:T(8,128)(2,1)S(1)} %multiply_convert_fusion), channel_id=1, source_target_pairs={{0,4},{4,8},{8,12},{12,16},{16,20},{20,24},{24,28},{28,0},{1,5},{5... | collective-permute-start | bytes 196616 | tf_op jit(solution)/shard_map/ppermute | solution.py:461
  29.2 2.3 %copy-start.8 = (bf16[256,512]{1,0:T(8,128)(2,1)S(1)}, bf16[256,512]{1,0:T(8,128)(2,1)}, u32[]{:S(2)}) copy-start(bf16[256,512]{1,0:T(8,128)(2,1)} %get-tuple-element.92) | copy-start | bytes 786436
  29.2 2.3 %copy-start.7 = (bf16[256,512]{1,0:T(8,128)(2,1)S(1)}, bf16[256,512]{1,0:T(8,128)(2,1)}, u32[]{:S(2)}) copy-start(bf16[256,512]{1,0:T(8,128)(2,1)} %get-tuple-element.93) | copy-start | bytes 786436
  31.4 2.2 %collective-permute-start.4 = (bf16[136,1024]{1,0:T(8,128)(2,1)}, bf16[136,1024]{1,0:T(8,128)(2,1)S(1)}, u32[]{:S(2)}, u32[]{:S(2)}) collective-permute-start(bf16[136,1024]{1,0:T(8,128)(2,1)} %get-tuple-element.80), channel_id=1, source_target_pairs={{0,4},{4,0},{8,12},{12,8},{16,20},{20,16},{24,28},{28,24},{1,5},{5... | collective-permute-start | bytes 835592 | tf_op jit(solution)/shard_map/ppermute | solution.py:562
  31.4 18.3 %collective-permute-start.15 = (bf16[256,512]{1,0:T(8,128)(2,1)S(1)}, bf16[256,512]{1,0:T(8,128)(2,1)S(1)}, u32[]{:S(2)}, u32[]{:S(2)}) collective-permute-start(bf16[256,512]{1,0:T(8,128)(2,1)S(1)} %copy-done.8), channel_id=1, source_target_pairs={{0,1},{1,2},{2,3},{3,0},{4,5},{5,6},{6,7},{7,4},{8,9},{9,10},{10,1... | collective-permute-start | bytes 786440 | tf_op jit(solution)/shard_map/ppermute | solution.py:533
  31.5 21.4 %collective-permute-start.16 = (bf16[256,512]{1,0:T(8,128)(2,1)S(1)}, bf16[256,512]{1,0:T(8,128)(2,1)S(1)}, u32[]{:S(2)}, u32[]{:S(2)}) collective-permute-start(bf16[256,512]{1,0:T(8,128)(2,1)S(1)} %copy-done.7), channel_id=1, source_target_pairs={{0,2},{1,3},{2,0},{3,1},{4,6},{5,7},{6,4},{7,5},{8,10},{9,11},{10,... | collective-permute-start | bytes 786440 | tf_op jit(solution)/shard_map/ppermute | solution.py:533
  33.7 7.1 %copy-start.6 = (bf16[256,512]{1,0:T(8,128)(2,1)S(1)}, bf16[256,512]{1,0:T(8,128)(2,1)}, u32[]{:S(2)}) copy-start(bf16[256,512]{1,0:T(8,128)(2,1)} %get-tuple-element.94) | copy-start | bytes 786436
  33.7 11.0 %copy-start = (bf16[256,512]{1,0:T(8,128)(2,1)S(1)}, bf16[256,512]{1,0:T(8,128)(2,1)}, u32[]{:S(2)}) copy-start(bf16[256,512]{1,0:T(8,128)(2,1)} %get-tuple-element.88.refs_8_) | copy-start | bytes 786436
  35.9 4.8 %collective-permute-start.5 = (bf16[48,1024]{1,0:T(8,128)(2,1)}, bf16[48,1024]{1,0:T(8,128)(2,1)S(1)}, u32[]{:S(2)}, u32[]{:S(2)}) collective-permute-start(bf16[48,1024]{1,0:T(8,128)(2,1)} %get-tuple-element.85), channel_id=1, source_target_pairs={{0,8},{4,12},{8,0},{12,4},{16,24},{20,28},{24,16},{28,20},{1,9},{5... | collective-permute-start | bytes 294920 | tf_op jit(solution)/shard_map/ppermute | solution.py:433
  37.4 5.9 %collective-permute-start.6 = (bf16[48,1024]{1,0:T(8,128)(2,1)}, bf16[48,1024]{1,0:T(8,128)(2,1)S(1)}, u32[]{:S(2)}, u32[]{:S(2)}) collective-permute-start(bf16[48,1024]{1,0:T(8,128)(2,1)} %get-tuple-element.86), channel_id=1, source_target_pairs={{0,16},{4,20},{8,24},{12,28},{16,0},{20,4},{24,8},{28,12},{1,17},{... | collective-permute-start | bytes 294920 | tf_op jit(solution)/shard_map/ppermute | solution.py:433
  38.9 5.7 %collective-permute-start.7 = (bf16[48,1024]{1,0:T(8,128)(2,1)}, bf16[48,1024]{1,0:T(8,128)(2,1)S(1)}, u32[]{:S(2)}, u32[]{:S(2)}) collective-permute-start(bf16[48,1024]{1,0:T(8,128)(2,1)} %get-tuple-element.87), channel_id=1, source_target_pairs={{0,24},{4,28},{8,16},{12,20},{16,8},{20,12},{24,0},{28,4},{1,25},{... | collective-permute-start | bytes 294920 | tf_op jit(solution)/shard_map/ppermute | solution.py:433
  40.7 20.3 %collective-permute-start.17 = (bf16[256,512]{1,0:T(8,128)(2,1)S(1)}, bf16[256,512]{1,0:T(8,128)(2,1)S(1)}, u32[]{:S(2)}, u32[]{:S(2)}) collective-permute-start(bf16[256,512]{1,0:T(8,128)(2,1)S(1)} %copy-done.6), channel_id=1, source_target_pairs={{0,3},{1,0},{2,1},{3,2},{4,7},{5,4},{6,5},{7,6},{8,11},{9,8},{10,9... | collective-permute-start | bytes 786440 | tf_op jit(solution)/shard_map/ppermute | solution.py:533
  43.3 11.1 %collective-permute-start.18 = (bf16[256,256]{1,0:T(8,128)(2,1)}, bf16[256,256]{1,0:T(8,128)(2,1)S(1)}, u32[]{:S(2)}, u32[]{:S(2)}) collective-permute-start(bf16[256,256]{1,0:T(8,128)(2,1)} %get-tuple-element.99), channel_id=1, source_target_pairs={{0,28},{4,0},{8,4},{12,8},{16,12},{20,16},{24,20},{28,24},{1,29},{... | collective-permute-start | bytes 393224 | tf_op jit(solution)/shard_map/ppermute | solution.py:583
  48.5 5.9 %collective-permute-start.13 = (bf16[40,1024]{1,0:T(8,128)(2,1)}, bf16[40,1024]{1,0:T(8,128)(2,1)S(1)}, u32[]{:S(2)}, u32[]{:S(2)}) collective-permute-start(bf16[40,1024]{1,0:T(8,128)(2,1)} %get-tuple-element.90.refs_0_), channel_id=1, source_target_pairs={{0,24},{4,28},{8,16},{12,20},{16,8},{20,12},{24,0},{28,4},{1,25},{... | collective-permute-start | bytes 245768 | tf_op jit(solution)/shard_map/ppermute | solution.py:440
  49.7 5.7 %collective-permute-start.11 = (bf16[40,1024]{1,0:T(8,128)(2,1)}, bf16[40,1024]{1,0:T(8,128)(2,1)S(1)}, u32[]{:S(2)}, u32[]{:S(2)}) collective-permute-start(bf16[40,1024]{1,0:T(8,128)(2,1)} %get-tuple-element.90.refs_0_), channel_id=1, source_target_pairs={{0,16},{4,20},{8,24},{12,28},{16,0},{20,4},{24,8},{28,12},{1,17},{... | collective-permute-start | bytes 245768 | tf_op jit(solution)/shard_map/ppermute | solution.py:440
  52.9 4.7 %collective-permute-start.9 = (bf16[40,1024]{1,0:T(8,128)(2,1)}, bf16[40,1024]{1,0:T(8,128)(2,1)S(1)}, u32[]{:S(2)}, u32[]{:S(2)}) collective-permute-start(bf16[40,1024]{1,0:T(8,128)(2,1)} %get-tuple-element.90.refs_0_), channel_id=1, source_target_pairs={{0,8},{4,12},{8,0},{12,4},{16,24},{20,28},{24,16},{28,20},{1,9},{5... | collective-permute-start | bytes 245768 | tf_op jit(solution)/shard_map/ppermute | solution.py:440
  54.4 6.7 %collective-permute-start.8 = (bf16[40,1024]{1,0:T(8,128)(2,1)}, bf16[40,1024]{1,0:T(8,128)(2,1)S(1)}, u32[]{:S(2)}, u32[]{:S(2)}) collective-permute-start(bf16[40,1024]{1,0:T(8,128)(2,1)} %get-tuple-element.90.refs_0_), channel_id=1, source_target_pairs={{0,4},{4,0},{8,12},{12,8},{16,20},{20,16},{24,28},{28,24},{1,5},{5... | collective-permute-start | bytes 245768 | tf_op jit(solution)/shard_map/ppermute | solution.py:440
  54.4 6.7 %collective-permute-start.14 = (bf16[40,1024]{1,0:T(8,128)(2,1)S(1)}, bf16[40,1024]{1,0:T(8,128)(2,1)S(1)}, u32[]{:S(2)}, u32[]{:S(2)}) collective-permute-start(bf16[40,1024]{1,0:T(8,128)(2,1)S(1)} %collective-permute-done.13.refs_6_), channel_id=1, source_target_pairs={{0,4},{4,0},{8,12},{12,8},{16,20},{20,16},{24,28},{28,24},{1,5},{5... | collective-permute-start | bytes 245768 | tf_op jit(solution)/shard_map/ppermute | solution.py:442
  55.4 5.7 %collective-permute-start.12 = (bf16[40,1024]{1,0:T(8,128)(2,1)S(1)}, bf16[40,1024]{1,0:T(8,128)(2,1)S(1)}, u32[]{:S(2)}, u32[]{:S(2)}) collective-permute-start(bf16[40,1024]{1,0:T(8,128)(2,1)S(1)} %collective-permute-done.11.refs_4_), channel_id=1, source_target_pairs={{0,4},{4,0},{8,12},{12,8},{16,20},{20,16},{24,28},{28,24},{1,5},{5... | collective-permute-start | bytes 245768 | tf_op jit(solution)/shard_map/ppermute | solution.py:442
  57.6 3.5 %collective-permute-start.10 = (bf16[40,1024]{1,0:T(8,128)(2,1)S(1)}, bf16[40,1024]{1,0:T(8,128)(2,1)S(1)}, u32[]{:S(2)}, u32[]{:S(2)}) collective-permute-start(bf16[40,1024]{1,0:T(8,128)(2,1)S(1)} %collective-permute-done.9.refs_2_), channel_id=1, source_target_pairs={{0,4},{4,0},{8,12},{12,8},{16,20},{20,16},{24,28},{28,24},{1,5},{5... | collective-permute-start | bytes 245768 | tf_op jit(solution)/shard_map/ppermute | solution.py:442
  57.6 3.6 %copy-start.1 = (bf16[256,512]{1,0:T(8,128)(2,1)S(1)}, bf16[256,512]{1,0:T(8,128)(2,1)}, u32[]{:S(2)}) copy-start(bf16[256,512]{1,0:T(8,128)(2,1)} %get-tuple-element.91.refs_8_) | copy-start | bytes 786436
  57.6 3.6 %copy-start.3 = (bf16[40,1024]{1,0:T(8,128)(2,1)S(1)}, bf16[40,1024]{1,0:T(8,128)(2,1)}, u32[]{:S(2)}) copy-start(bf16[40,1024]{1,0:T(8,128)(2,1)} %get-tuple-element.90.refs_0_) | copy-start | bytes 245764

commit v3 on v2

--- a/solution.py
+++ b/solution.py
@@ -10,6 +10,7 @@
 
 BLK = 128
 VMEM_LIMIT = 12 << 20
+PARTS = 2
 HIGHEST = lax.Precision.HIGHEST
 F32 = jnp.float32
 BF16 = jnp.bfloat16
@@ -363,10 +364,9 @@
         out[...] = filter_rows
 
 
-def fifth_kernel(size, ctx_size, p2_grad, turned_grad, beside, edge, q2_grad, gated, conv, k2, k1, v1, short, q2_out, k2_out, q1_out, k1_out, v1_out, next_grad):
+def fifth_kernel(size, ctx_size, p2_grad, turned_grad, beside, edge, gated, conv, k2, k1, v1, short, k2_out, q1_out, k1_out, v1_out, next_grad):
     groups = short.shape[0]
     count = p2_grad.shape[1] // BLK
-    q2_out[...] = q2_grad[...]
     p2g = p2_grad[...].astype(F32)
     k2_out[...] = (p2g * gated[...].astype(F32)).astype(BF16)
     q1_out[...] = (p2g * k2[...].astype(F32) * conv[...].astype(F32)).astype(BF16)
@@ -399,20 +399,33 @@
     mixed[...] = summed.astype(BF16)
 
 
-def call(kernel, outs, *args, held=(), far=(), scratch=(), name):
+def call(kernel, outs, *args, held=(), far=(), scratch=(), parts=1, name):
     size = sum(math.prod(a.shape) * a.dtype.itemsize for a in args)
     size += sum(math.prod(s) * jnp.dtype(t).itemsize for s, t in outs)
     args = [pltpu.with_memory_space_constraint(a, pltpu.HBM) if i in far else a for i, a in enumerate(args)]
+    if parts > 1:
+        def cut(shape):
+            rest = len(shape) - 1
+            return pl.BlockSpec((shape[0] // parts, *shape[1:]), lambda i: (i,) + (0,) * rest)
+
+        extra = dict(grid=(parts,))
+        in_specs = [cut(a.shape) for a in args]
+        out_specs = [cut(s) for s, t in outs]
+    else:
+        extra = {}
+        in_specs = [
+            pl.BlockSpec(memory_space=pltpu.HBM if name == "tables" and i > 2 else pltpu.VMEM)
+            for i in range(len(args))
+        ]
+        out_specs = [pl.BlockSpec(memory_space=pltpu.VMEM)] * len(outs)
     results = pl.pallas_call(
         kernel,
         out_shape=[
             pltpu.VMEM(s, t) if i in held else pltpu.HBM(s, t) for i, (s, t) in enumerate(outs)
         ],
-        in_specs=[
-            pl.BlockSpec(memory_space=pltpu.HBM if name == "tables" and i > 2 else pltpu.VMEM)
-            for i in range(len(args))
-        ],
-        out_specs=[pl.BlockSpec(memory_space=pltpu.VMEM)] * len(outs),
+        in_specs=in_specs,
+        out_specs=out_specs,
+        **extra,
         scratch_shapes=list(scratch),
         cost_estimate=pl.CostEstimate(flops=0, bytes_accessed=size, transcendentals=0),
         compiler_params=pltpu.CompilerParams(vmem_limit_bytes=VMEM_LIMIT),
@@ -509,7 +522,7 @@
         long,
         close,
         rate_t,
-        held=(2, 3, 5, 6),
+        held=(2, 5, 6),
         scratch=[pltpu.VMEM((chans, length), BF16)],
         name="first",
     )
@@ -593,7 +606,7 @@
         late_q1,
         late_k2,
         mirrored,
-        far=(0, n_ctx // 2) if fused else (),
+        far=(0, n_ctx // 2, n_ctx // 2 + 7) if fused else (),
         name="fourth",
     )
     scale = 1.0 / math.sqrt(length * n_ctx)
@@ -601,22 +614,22 @@
         final = gather(last, n_ctx)
     else:
         weight_total, filter_total = lax.psum((sent_back[1], last), "ctx")
-    q2_out, k2_out, q1_out, k1_out, v1_out = call(
+    k2_out, q1_out, k1_out, v1_out = call(
         functools.partial(fifth_kernel, size, n_ctx),
-        [stream] * 5,
+        [stream] * 4,
         p2_grad,
         turned_grad,
         beside,
         next_edge,
-        q2_grad,
         gated,
         conv,
         late_k2,
         late_k1,
         late_v1,
         short,
-        far=(0, 1, 2, 4, 5, 6),
-        scratch=[pltpu.VMEM((chans, BLK), BF16)],
+        far=(0, 1, 2, 4, 5),
+        scratch=[pltpu.VMEM((chans // PARTS, BLK), BF16)],
+        parts=PARTS,
         name="fifth",
     )
     if fused:
@@ -632,7 +645,7 @@
         weight_grad = scale * weight_total
         mixed = sum(p.astype(F32) for p in mixed_parts).astype(BF16)
         filter_grad = scale * filter_total
-    return (mixed, q1_out, k1_out, v1_out, q2_out, k2_out, weight_grad, filter_grad)
+    return (mixed, q1_out, k1_out, v1_out, q2_grad, k2_out, weight_grad, filter_grad)
 
 
 def solution(mesh):

time: 62.9 us -> 62.5 us (level)
  no operation moved by 1% of the time
where the time goes in v3:
time: 62.5 us; the launch traced here: 61.9 us
  Pallas kernels  18.7 us (30%)
  starting transfers between devices  18.4 us (29%)
  waiting for transfers between devices  14.4 us (23%)
  blocking collectives  8.11 us (13%)
  other arithmetic  0.91 us (1%)
  between operations  0.8 us (1%)
    pallas_call x8, Pallas kernels, call(): pl.pallas_call(kernel, out_shape=[pltpu.VMEM(s, t) if i in held else pltp...  18.7 us
    all_to_all x1, blocking collectives, on_device(): states = lax.all_to_all(sent, 'ctx', 0, 0, tiled=True)  8.11 us
    ppermute x3, starting transfers between devices, on_device(): grads.append(lax.ppermute(out_grad, 'ch', around(n_ch, k)))  6.14 us
    ppermute x3, waiting for transfers between devices, on_device(): grads.append(lax.ppermute(out_grad, 'ch', around(n_ch, k)))  4.89 us
    ppermute x3, starting transfers between devices, on_device(): mixed_parts.append(lax.ppermute(parts[k], 'ch', around(n_ch, k)))  4.13 us
    ppermute x4, starting transfers between devices, gather(): out[k] = lax.ppermute(block, 'ctx', [(i, i ^ k) for i in range(count)])  3.6 us
    ppermute x3, starting transfers between devices, exchange(): lax.ppermute(blocks[i], 'ctx', [(d, d ^ 2 * i) for d in range(count)])  3.49 us
    ppermute x3, waiting for transfers between devices, exchange(): lax.ppermute(blocks[i], 'ctx', [(d, d ^ 2 * i) for d in range(count)])  2.81 us
  transfers between devices with their start and end apart: 19, of which 8 were waited for; matrix products, arithmetic and copies ran while one was open for 1% of the time, Pallas kernels for 25%

profile of v3, /device:TPU:0, one launch (start us, length us, event | category | flops | bytes accessed | tf_op | source)
XLA Modules:
  0.0 61.9 jit_solution(7136972329269468307)
XLA Ops:
  0.6 0.0 copy-start.2
  0.6 0.0 copy-start.5
  0.7 3.1 %collective-permute-start = (bf16[256,512]{1,0:T(8,128)(2,1)}, bf16[256,512]{1,0:T(8,128)(2,1)S(1)}, u32[]{:S(2)}, u32[]{:S(2)}) collective-permute-start(bf16[256,512]{1,0:T(8,128)(2,1)} %refs_8_.1), channel_id=1, source_target_pairs={{0,1},{1,2},{2,3},{3,0},{4,5},{5,6},{6,7},{7,4},{8,9},{9,10},{10,1... | collective-permute-start | bytes 786440 | tf_op jit(solution)/shard_map/ppermute | solution.py:477
  3.8 2.1 %collective-permute-start.2 = (bf16[256,512]{1,0:T(8,128)(2,1)}, bf16[256,512]{1,0:T(8,128)(2,1)S(1)}, u32[]{:S(2)}, u32[]{:S(2)}) collective-permute-start(bf16[256,512]{1,0:T(8,128)(2,1)} %refs_8_.1), channel_id=1, source_target_pairs={{0,3},{1,0},{2,1},{3,2},{4,7},{5,4},{6,5},{7,6},{8,11},{9,8},{10,9... | collective-permute-start | bytes 786440 | tf_op jit(solution)/shard_map/ppermute | solution.py:477
  5.9 0.9 %collective-permute-start.1 = (bf16[256,512]{1,0:T(8,128)(2,1)}, bf16[256,512]{1,0:T(8,128)(2,1)S(1)}, u32[]{:S(2)}, u32[]{:S(2)}) collective-permute-start(bf16[256,512]{1,0:T(8,128)(2,1)} %refs_8_.1), channel_id=1, source_target_pairs={{0,2},{1,3},{2,0},{3,1},{4,6},{5,7},{6,4},{7,5},{8,10},{9,11},{10,... | collective-permute-start | bytes 786440 | tf_op jit(solution)/shard_map/ppermute | solution.py:477
  6.8 0.9 %multiply_convert_fusion = bf16[256,128]{1,0:T(8,128)(2,1)S(1)} fusion(bf16[256,512]{1,0:T(8,128)(2,1)} %v1.1, bf16[256,512]{1,0:T(8,128)(2,1)} %k1.1), kind=kLoop, calls=%fused_computation | loop fusion | flops 131072 | bytes 196608 | tf_op jit(solution)/shard_map/convert_element_type | solution.py:473
  7.7 0.0 copy-start.4
  7.7 0.1 collective-permute-start.3
  7.8 0.0 copy-done.2
  7.8 0.0 copy-done.5
  7.8 0.6 copy-done.4
  8.4 2.0 %shard_map.161 = (bf16[16,256,128]{2,1,0:T(8,128)(2,1)S(1)}, bf16[16,128,128]{2,1,0:T(8,128)(2,1)S(1)}, bf16[512,128]{1,0:T(8,128)(2,1)S(1)}, bf16[512,128]{1,0:...) custom-call(bf16[16,128]{1,0:T(8,128)(2,1)S(1)} %copy-done.4, ...), custom_call_target="tpu_custom_call" | custom-call | bytes 6264832 | tf_op jit(solution)/shard_map/pallas_call | solution.py:421
  10.4 1.9 %collective-permute-done.3.halo = bf16[256,128]{1,0:T(8,128)(2,1)S(1)} collective-permute-done((bf16[256,128]{1,0:T(8,128)(2,1)S(1)}, bf16[256,128]{1,0:T(8,128)(2,1)S(1)}, u32[]{:S(2)}, u32[]{:S(2)}) %collective-permute-start.3) | collective-permute-done | bytes 65568 | tf_op jit(solution)/shard_map/ppermute | solution.py:474
  12.3 1.5 %shard_map.162 = (bf16[256,512]{1,0:T(8,128)(2,1)}, bf16[256,512]{1,0:T(8,128)(2,1)}, bf16[256,512]{1,0:T(8,128)(2,1)S(1)}, bf16[256,640]{1,0:T(8,128)(2,1)}, bf...) custom-call(bf16[256,128]{1,0:T(8,128)(2,1)S(1)} %collective-permute-done.3.halo, ...), custom_call_target="tpu_custom_call" | custom-call | bytes 4210688 | tf_op jit(solution)/shard_map/pallas_call | solution.py:421
  13.9 8.1 %all_to_all.5.states = f32[8,16,256]{2,1,0:T(8,128)S(1)} all-to-all(f32[8,16,256]{2,1,0:T(8,128)S(1)} %get-tuple-element.69), channel_id=1, replica_groups=mesh['ctx'=8,'ch'=4] {'ctx'}, dimensions={0} | all-to-all | bytes 262144 | tf_op jit(solution)/shard_map/all_to_all | solution.py:529
  22.0 2.3 %shard_map.163 = (bf16[256,512]{1,0:T(8,128)(2,1)S(1)}, bf16[256,512]{1,0:T(8,128)(2,1)S(1)}, bf16[256,512]{1,0:T(8,128)(2,1)}, bf16[256,512]{1,0:T(8,128)(2,1)}...) custom-call(f32[8,16,256]{2,1,0:T(8,128)S(1)} %all_to_all.5.states, f32[4,16,256]{2,1,0:T(8,128)S(1)} %get-tuple-element.70.sub, ...), custom_call_target="tpu_custom_call" | custom-call | bytes 3047424 | tf_op jit(solution)/shard_map/pallas_call | solution.py:421
  24.3 0.0 collective-permute-done.refs_1_
  24.3 0.0 collective-permute-done.2.refs_3_
  24.3 4.9 %collective-permute-done.1.refs_2_ = bf16[256,512]{1,0:T(8,128)(2,1)S(1)} collective-permute-done((bf16[256,512]{1,0:T(8,128)(2,1)}, bf16[256,512]{1,0:T(8,128)(2,1)S(1)}, u32[]{:S(2)}, u32[]{:S(2)}) %collective-permute-start.1) | collective-permute-done | bytes 262176 | tf_op jit(solution)/shard_map/ppermute | solution.py:477
  29.2 0.0 copy-start.8
  29.2 0.0 copy-start.7
  29.2 2.3 %shard_map.164 = (bf16[256,512]{1,0:T(8,128)(2,1)}, bf16[256,512]{1,0:T(8,128)(2,1)}, f32[4,16,256]{2,1,0:T(8,128)}, bf16[256,128]{1,0:T(8,128)(2,1)}, bf16[128,...) custom-call(bf16[256,512]{1,0:T(8,128)(2,1)S(1)} %get-tuple-element.58.refs_0_, ...), custom_call_target="tpu_custom_call" | custom-call | bytes 4243456 | tf_op jit(solution)/shard_map/pallas_call | solution.py:421
  31.4 0.0 collective-permute-start.4
  31.4 0.0 copy-done.8
  31.4 0.0 collective-permute-start.15
  31.5 0.0 copy-done.7
  31.5 2.2 %collective-permute-start.16 = (bf16[256,512]{1,0:T(8,128)(2,1)S(1)}, bf16[256,512]{1,0:T(8,128)(2,1)S(1)}, u32[]{:S(2)}, u32[]{:S(2)}) collective-permute-start(bf16[256,512]{1,0:T(8,128)(2,1)S(1)} %copy-done.7), channel_id=1, source_target_pairs={{0,2},{1,3},{2,0},{3,1},{4,6},{5,7},{6,4},{7,5},{8,10},{9,11},{10,... | collective-permute-start | bytes 786440 | tf_op jit(solution)/shard_map/ppermute | solution.py:546
  33.6 0.0 collective-permute-done.4.got
  33.6 0.0 copy-start.6
  33.6 0.0 copy-start
  33.7 2.3 %shard_map.165 = (bf16[256,256]{1,0:T(8,128)(2,1)}, bf16[48,1024]{1,0:T(8,128)(2,1)}, bf16[48,1024]{1,0:T(8,128)(2,1)}, bf16[48,1024]{1,0:T(8,128)(2,1)}, bf16[48,1024]{1,0:T(8,128)(2,1)}) custom-call(bf16[128,1024]{1,0:T(8,128)(2,1)} %get-tuple-element.77.kept, bf16[8,1024]{1,0:T(8,128)(2,1)} %get-tuple-element.78.own, ...), custom_call_target="tpu_custom_call" | custom-call | bytes 1311744 | tf_op jit(solution)/shard_map/pallas_call | solution.py:421
  35.9 1.5 %collective-permute-start.5 = (bf16[48,1024]{1,0:T(8,128)(2,1)}, bf16[48,1024]{1,0:T(8,128)(2,1)S(1)}, u32[]{:S(2)}, u32[]{:S(2)}) collective-permute-start(bf16[48,1024]{1,0:T(8,128)(2,1)} %get-tuple-element.84), channel_id=1, source_target_pairs={{0,8},{4,12},{8,0},{12,4},{16,24},{20,28},{24,16},{28,20},{1,9},{5... | collective-permute-start | bytes 294920 | tf_op jit(solution)/shard_map/ppermute | solution.py:446
  37.4 1.5 %collective-permute-start.6 = (bf16[48,1024]{1,0:T(8,128)(2,1)}, bf16[48,1024]{1,0:T(8,128)(2,1)S(1)}, u32[]{:S(2)}, u32[]{:S(2)}) collective-permute-start(bf16[48,1024]{1,0:T(8,128)(2,1)} %get-tuple-element.85), channel_id=1, source_target_pairs={{0,16},{4,20},{8,24},{12,28},{16,0},{20,4},{24,8},{28,12},{1,17},{... | collective-permute-start | bytes 294920 | tf_op jit(solution)/shard_map/ppermute | solution.py:446
  38.9 0.5 collective-permute-start.7
  39.4 1.3 %collective-permute-done.5.refs_1_ = bf16[48,1024]{1,0:T(8,128)(2,1)S(1)} collective-permute-done((bf16[48,1024]{1,0:T(8,128)(2,1)}, bf16[48,1024]{1,0:T(8,128)(2,1)S(1)}, u32[]{:S(2)}, u32[]{:S(2)}) %collective-permute-start.5) | collective-permute-done | bytes 98336 | tf_op jit(solution)/shard_map/ppermute | solution.py:446
  40.7 0.0 copy-done.6
  40.7 1.9 %collective-permute-start.17 = (bf16[256,512]{1,0:T(8,128)(2,1)S(1)}, bf16[256,512]{1,0:T(8,128)(2,1)S(1)}, u32[]{:S(2)}, u32[]{:S(2)}) collective-permute-start(bf16[256,512]{1,0:T(8,128)(2,1)S(1)} %copy-done.6), channel_id=1, source_target_pairs={{0,3},{1,0},{2,1},{3,2},{4,7},{5,4},{6,5},{7,6},{8,11},{9,8},{10,9... | collective-permute-start | bytes 786440 | tf_op jit(solution)/shard_map/ppermute | solution.py:546
  42.7 0.6 %collective-permute-done.6.refs_2_ = bf16[48,1024]{1,0:T(8,128)(2,1)S(1)} collective-permute-done((bf16[48,1024]{1,0:T(8,128)(2,1)}, bf16[48,1024]{1,0:T(8,128)(2,1)S(1)}, u32[]{:S(2)}, u32[]{:S(2)}) %collective-permute-start.6) | collective-permute-done | bytes 98336 | tf_op jit(solution)/shard_map/ppermute | solution.py:446
  43.3 0.5 collective-permute-start.18
  43.8 0.8 %collective-permute-done.7.refs_3_ = bf16[48,1024]{1,0:T(8,128)(2,1)S(1)} collective-permute-done((bf16[48,1024]{1,0:T(8,128)(2,1)}, bf16[48,1024]{1,0:T(8,128)(2,1)S(1)}, u32[]{:S(2)}, u32[]{:S(2)}) %collective-permute-start.7) | collective-permute-done | bytes 98336 | tf_op jit(solution)/shard_map/ppermute | solution.py:446
  44.6 0.0 copy-done
  44.7 4.0 %shard_map.166 = (f32[256,128]{1,0:T(8,128)}, bf16[256,512]{1,0:T(8,128)(2,1)}, bf16[256,512]{1,0:T(8,128)(2,1)}, bf16[40,1024]{1,0:T(8,128)(2,1)}) custom-call(bf16[48,1024]{1,0:T(8,128)(2,1)} %get-tuple-element.83.refs_0_, bf16[48,1024]{1,0:T(8,128)(2,1)S(1)} %collective-permute-done.5.refs_1_, bf16[48,1024]{1,0:T(8,128)(2,1)S(1)} %collective-permute-done.6.refs_2_, ...), custom_call_target="tpu_custom_call" | custom-call | bytes 2343936 | tf_op jit(solution)/shard_map/pallas_call | solution.py:421
  48.6 1.2 %collective-permute-start.13 = (bf16[40,1024]{1,0:T(8,128)(2,1)}, bf16[40,1024]{1,0:T(8,128)(2,1)S(1)}, u32[]{:S(2)}, u32[]{:S(2)}) collective-permute-start(bf16[40,1024]{1,0:T(8,128)(2,1)} %get-tuple-element.89.refs_0_), channel_id=1, source_target_pairs={{0,24},{4,28},{8,16},{12,20},{16,8},{20,12},{24,0},{28,4},{1,25},{... | collective-permute-start | bytes 245768 | tf_op jit(solution)/shard_map/ppermute | solution.py:453
  49.8 0.0 collective-permute-done.15.refs_9_
  49.8 0.9 %collective-permute-start.11 = (bf16[40,1024]{1,0:T(8,128)(2,1)}, bf16[40,1024]{1,0:T(8,128)(2,1)S(1)}, u32[]{:S(2)}, u32[]{:S(2)}) collective-permute-start(bf16[40,1024]{1,0:T(8,128)(2,1)} %get-tuple-element.89.refs_0_), channel_id=1, source_target_pairs={{0,16},{4,20},{8,24},{12,28},{16,0},{20,4},{24,8},{28,12},{1,17},{... | collective-permute-start | bytes 245768 | tf_op jit(solution)/shard_map/ppermute | solution.py:453
  50.8 2.1 %collective-permute-done.16.refs_10_ = bf16[256,512]{1,0:T(8,128)(2,1)S(1)} collective-permute-done((bf16[256,512]{1,0:T(8,128)(2,1)S(1)}, bf16[256,512]{1,0:T(8,128)(2,1)S(1)}, u32[]{:S(2)}, u32[]{:S(2)}) %collective-permute-start.16) | collective-permute-done | bytes 262176 | tf_op jit(solution)/shard_map/ppermute | solution.py:546
  52.9 1.5 %collective-permute-start.9 = (bf16[40,1024]{1,0:T(8,128)(2,1)}, bf16[40,1024]{1,0:T(8,128)(2,1)S(1)}, u32[]{:S(2)}, u32[]{:S(2)}) collective-permute-start(bf16[40,1024]{1,0:T(8,128)(2,1)} %get-tuple-element.89.refs_0_), channel_id=1, source_target_pairs={{0,8},{4,12},{8,0},{12,4},{16,24},{20,28},{24,16},{28,20},{1,9},{5... | collective-permute-start | bytes 245768 | tf_op jit(solution)/shard_map/ppermute | solution.py:453
  54.4 0.0 collective-permute-done.18.edge
  54.4 0.0 collective-permute-start.8
  54.4 0.0 collective-permute-done.13.refs_6_
  54.4 0.5 collective-permute-start.14
  54.9 0.6 collective-permute-done.11.refs_4_
  55.5 0.0 collective-permute-start.12
  55.5 2.1 %collective-permute-done.9.refs_2_ = bf16[40,1024]{1,0:T(8,128)(2,1)S(1)} collective-permute-done((bf16[40,1024]{1,0:T(8,128)(2,1)}, bf16[40,1024]{1,0:T(8,128)(2,1)S(1)}, u32[]{:S(2)}, u32[]{:S(2)}) %collective-permute-start.9) | collective-permute-done | bytes 81952 | tf_op jit(solution)/shard_map/ppermute | solution.py:453
  57.6 0.0 collective-permute-start.10
  57.6 3.1 %shard_map.168 = (bf16[256,512]{1,0:T(8,128)(2,1)}, bf16[256,512]{1,0:T(8,128)(2,1)}, bf16[256,512]{1,0:T(8,128)(2,1)}, bf16[256,512]{1,0:T(8,128)(2,1)}) custom-call(bf16[256,512]{1,0:T(8,128)(2,1)} %get-tuple-element.95.p2_grad, bf16[256,512]{1,0:T(8,128)(2,1)} %get-tuple-element.96.turned_grad, f32[256,128]{1,0:T(8,128)} %get-tuple-element.97.beside, ...), custom_call_target="tpu_custom_call" | custom-call | bytes 4194304 | tf_op jit(solution)/shard_map/pallas_call | solution.py:421
  60.7 0.0 collective-permute-done.17.refs_11_
  60.7 0.0 collective-permute-done.8.refs_1_
  60.7 0.0 collective-permute-done.14.refs_7_
  60.7 0.0 collective-permute-done.12.refs_5_
  60.7 0.0 collective-permute-done.10.refs_3_
  60.7 0.0 copy-done.1
  60.7 0.0 copy-done.3
  60.7 1.2 %shard_map.167 = (f32[8,32,1024]{2,1,0:T(8,128)}, f32[16,128]{1,0:T(8,128)}, bf16[256,512]{1,0:T(8,128)(2,1)}) custom-call(bf16[40,1024]{1,0:T(8,128)(2,1)S(1)} %copy-done.3, bf16[40,1024]{1,0:T(8,128)(2,1)S(1)} %collective-permute-done.8.refs_1_, bf16[40,1024]{1,0:T(8,128)(2,1)S(1)} %collective-permute-done.9.refs_2_, ...), custom_call_target="tpu_custom_call" | custom-call | bytes 3022848 | tf_op jit(solution)/shard_map/pallas_call | solution.py:421
  (3 shorter events, 0.0 us)
Async XLA Ops:
  0.6 7.1 %copy-start.2 = (f32[16,16]{1,0:T(8,128)S(1)}, f32[16,16]{1,0:T(8,128)}, u32[]{:S(2)}) copy-start(f32[16,16]{1,0:T(8,128)} %refs_7_.3) | copy-start | bytes 3076
  0.6 7.1 %copy-start.5 = (f32[16,16]{1,0:T(8,128)S(1)}, f32[16,16]{1,0:T(8,128)}, u32[]{:S(2)}) copy-start(f32[16,16]{1,0:T(8,128)} %param.18) | copy-start | bytes 3076
  0.7 23.6 %collective-permute-start = (bf16[256,512]{1,0:T(8,128)(2,1)}, bf16[256,512]{1,0:T(8,128)(2,1)S(1)}, u32[]{:S(2)}, u32[]{:S(2)}) collective-permute-start(bf16[256,512]{1,0:T(8,128)(2,1)} %refs_8_.1), channel_id=1, source_target_pairs={{0,1},{1,2},{2,3},{3,0},{4,5},{5,6},{6,7},{7,4},{8,9},{9,10},{10,1... | collective-permute-start | bytes 786440 | tf_op jit(solution)/shard_map/ppermute | solution.py:477
  3.8 20.5 %collective-permute-start.2 = (bf16[256,512]{1,0:T(8,128)(2,1)}, bf16[256,512]{1,0:T(8,128)(2,1)S(1)}, u32[]{:S(2)}, u32[]{:S(2)}) collective-permute-start(bf16[256,512]{1,0:T(8,128)(2,1)} %refs_8_.1), channel_id=1, source_target_pairs={{0,3},{1,0},{2,1},{3,2},{4,7},{5,4},{6,5},{7,6},{8,11},{9,8},{10,9... | collective-permute-start | bytes 786440 | tf_op jit(solution)/shard_map/ppermute | solution.py:477
  5.9 23.3 %collective-permute-start.1 = (bf16[256,512]{1,0:T(8,128)(2,1)}, bf16[256,512]{1,0:T(8,128)(2,1)S(1)}, u32[]{:S(2)}, u32[]{:S(2)}) collective-permute-start(bf16[256,512]{1,0:T(8,128)(2,1)} %refs_8_.1), channel_id=1, source_target_pairs={{0,2},{1,3},{2,0},{3,1},{4,6},{5,7},{6,4},{7,5},{8,10},{9,11},{10,... | collective-permute-start | bytes 786440 | tf_op jit(solution)/shard_map/ppermute | solution.py:477
  7.7 0.7 %copy-start.4 = (bf16[16,128]{1,0:T(8,128)(2,1)S(1)}, bf16[16,128]{1,0:T(8,128)(2,1)}, u32[]{:S(2)}) copy-start(bf16[16,128]{1,0:T(8,128)(2,1)} %refs_0_.1) | copy-start | bytes 12292
  7.7 4.6 %collective-permute-start.3 = (bf16[256,128]{1,0:T(8,128)(2,1)S(1)}, bf16[256,128]{1,0:T(8,128)(2,1)S(1)}, u32[]{:S(2)}, u32[]{:S(2)}) collective-permute-start(bf16[256,128]{1,0:T(8,128)(2,1)S(1)} %multiply_convert_fusion), channel_id=1, source_target_pairs={{0,4},{4,8},{8,12},{12,16},{16,20},{20,24},{24,28},{28,0},{1,5},{5... | collective-permute-start | bytes 196616 | tf_op jit(solution)/shard_map/ppermute | solution.py:474
  29.2 2.3 %copy-start.8 = (bf16[256,512]{1,0:T(8,128)(2,1)S(1)}, bf16[256,512]{1,0:T(8,128)(2,1)}, u32[]{:S(2)}) copy-start(bf16[256,512]{1,0:T(8,128)(2,1)} %get-tuple-element.91) | copy-start | bytes 786436
  29.2 2.3 %copy-start.7 = (bf16[256,512]{1,0:T(8,128)(2,1)S(1)}, bf16[256,512]{1,0:T(8,128)(2,1)}, u32[]{:S(2)}) copy-start(bf16[256,512]{1,0:T(8,128)(2,1)} %get-tuple-element.92) | copy-start | bytes 786436
  31.4 2.2 %collective-permute-start.4 = (bf16[136,1024]{1,0:T(8,128)(2,1)}, bf16[136,1024]{1,0:T(8,128)(2,1)S(1)}, u32[]{:S(2)}, u32[]{:S(2)}) collective-permute-start(bf16[136,1024]{1,0:T(8,128)(2,1)} %get-tuple-element.79), channel_id=1, source_target_pairs={{0,4},{4,0},{8,12},{12,8},{16,20},{20,16},{24,28},{28,24},{1,5},{5... | collective-permute-start | bytes 835592 | tf_op jit(solution)/shard_map/ppermute | solution.py:575
  31.4 18.4 %collective-permute-start.15 = (bf16[256,512]{1,0:T(8,128)(2,1)S(1)}, bf16[256,512]{1,0:T(8,128)(2,1)S(1)}, u32[]{:S(2)}, u32[]{:S(2)}) collective-permute-start(bf16[256,512]{1,0:T(8,128)(2,1)S(1)} %copy-done.8), channel_id=1, source_target_pairs={{0,1},{1,2},{2,3},{3,0},{4,5},{5,6},{6,7},{7,4},{8,9},{9,10},{10,1... | collective-permute-start | bytes 786440 | tf_op jit(solution)/shard_map/ppermute | solution.py:546
  31.5 21.4 %collective-permute-start.16 = (bf16[256,512]{1,0:T(8,128)(2,1)S(1)}, bf16[256,512]{1,0:T(8,128)(2,1)S(1)}, u32[]{:S(2)}, u32[]{:S(2)}) collective-permute-start(bf16[256,512]{1,0:T(8,128)(2,1)S(1)} %copy-done.7), channel_id=1, source_target_pairs={{0,2},{1,3},{2,0},{3,1},{4,6},{5,7},{6,4},{7,5},{8,10},{9,11},{10,... | collective-permute-start | bytes 786440 | tf_op jit(solution)/shard_map/ppermute | solution.py:546
  33.6 7.1 %copy-start.6 = (bf16[256,512]{1,0:T(8,128)(2,1)S(1)}, bf16[256,512]{1,0:T(8,128)(2,1)}, u32[]{:S(2)}) copy-start(bf16[256,512]{1,0:T(8,128)(2,1)} %get-tuple-element.93) | copy-start | bytes 786436
  33.6 11.0 %copy-start = (bf16[256,512]{1,0:T(8,128)(2,1)S(1)}, bf16[256,512]{1,0:T(8,128)(2,1)}, u32[]{:S(2)}) copy-start(bf16[256,512]{1,0:T(8,128)(2,1)} %get-tuple-element.87.refs_8_) | copy-start | bytes 786436
  35.9 4.8 %collective-permute-start.5 = (bf16[48,1024]{1,0:T(8,128)(2,1)}, bf16[48,1024]{1,0:T(8,128)(2,1)S(1)}, u32[]{:S(2)}, u32[]{:S(2)}) collective-permute-start(bf16[48,1024]{1,0:T(8,128)(2,1)} %get-tuple-element.84), channel_id=1, source_target_pairs={{0,8},{4,12},{8,0},{12,4},{16,24},{20,28},{24,16},{28,20},{1,9},{5... | collective-permute-start | bytes 294920 | tf_op jit(solution)/shard_map/ppermute | solution.py:446
  37.4 5.9 %collective-permute-start.6 = (bf16[48,1024]{1,0:T(8,128)(2,1)}, bf16[48,1024]{1,0:T(8,128)(2,1)S(1)}, u32[]{:S(2)}, u32[]{:S(2)}) collective-permute-start(bf16[48,1024]{1,0:T(8,128)(2,1)} %get-tuple-element.85), channel_id=1, source_target_pairs={{0,16},{4,20},{8,24},{12,28},{16,0},{20,4},{24,8},{28,12},{1,17},{... | collective-permute-start | bytes 294920 | tf_op jit(solution)/shard_map/ppermute | solution.py:446
  38.9 5.7 %collective-permute-start.7 = (bf16[48,1024]{1,0:T(8,128)(2,1)}, bf16[48,1024]{1,0:T(8,128)(2,1)S(1)}, u32[]{:S(2)}, u32[]{:S(2)}) collective-permute-start(bf16[48,1024]{1,0:T(8,128)(2,1)} %get-tuple-element.86), channel_id=1, source_target_pairs={{0,24},{4,28},{8,16},{12,20},{16,8},{20,12},{24,0},{28,4},{1,25},{... | collective-permute-start | bytes 294920 | tf_op jit(solution)/shard_map/ppermute | solution.py:446
  40.7 19.9 %collective-permute-start.17 = (bf16[256,512]{1,0:T(8,128)(2,1)S(1)}, bf16[256,512]{1,0:T(8,128)(2,1)S(1)}, u32[]{:S(2)}, u32[]{:S(2)}) collective-permute-start(bf16[256,512]{1,0:T(8,128)(2,1)S(1)} %copy-done.6), channel_id=1, source_target_pairs={{0,3},{1,0},{2,1},{3,2},{4,7},{5,4},{6,5},{7,6},{8,11},{9,8},{10,9... | collective-permute-start | bytes 786440 | tf_op jit(solution)/shard_map/ppermute | solution.py:546
  43.3 11.1 %collective-permute-start.18 = (bf16[256,256]{1,0:T(8,128)(2,1)}, bf16[256,256]{1,0:T(8,128)(2,1)S(1)}, u32[]{:S(2)}, u32[]{:S(2)}) collective-permute-start(bf16[256,256]{1,0:T(8,128)(2,1)} %get-tuple-element.98), channel_id=1, source_target_pairs={{0,28},{4,0},{8,4},{12,8},{16,12},{20,16},{24,20},{28,24},{1,29},{... | collective-permute-start | bytes 393224 | tf_op jit(solution)/shard_map/ppermute | solution.py:596
  48.6 5.8 %collective-permute-start.13 = (bf16[40,1024]{1,0:T(8,128)(2,1)}, bf16[40,1024]{1,0:T(8,128)(2,1)S(1)}, u32[]{:S(2)}, u32[]{:S(2)}) collective-permute-start(bf16[40,1024]{1,0:T(8,128)(2,1)} %get-tuple-element.89.refs_0_), channel_id=1, source_target_pairs={{0,24},{4,28},{8,16},{12,20},{16,8},{20,12},{24,0},{28,4},{1,25},{... | collective-permute-start | bytes 245768 | tf_op jit(solution)/shard_map/ppermute | solution.py:453
  49.8 5.7 %collective-permute-start.11 = (bf16[40,1024]{1,0:T(8,128)(2,1)}, bf16[40,1024]{1,0:T(8,128)(2,1)S(1)}, u32[]{:S(2)}, u32[]{:S(2)}) collective-permute-start(bf16[40,1024]{1,0:T(8,128)(2,1)} %get-tuple-element.89.refs_0_), channel_id=1, source_target_pairs={{0,16},{4,20},{8,24},{12,28},{16,0},{20,4},{24,8},{28,12},{1,17},{... | collective-permute-start | bytes 245768 | tf_op jit(solution)/shard_map/ppermute | solution.py:453
  52.9 4.7 %collective-permute-start.9 = (bf16[40,1024]{1,0:T(8,128)(2,1)}, bf16[40,1024]{1,0:T(8,128)(2,1)S(1)}, u32[]{:S(2)}, u32[]{:S(2)}) collective-permute-start(bf16[40,1024]{1,0:T(8,128)(2,1)} %get-tuple-element.89.refs_0_), channel_id=1, source_target_pairs={{0,8},{4,12},{8,0},{12,4},{16,24},{20,28},{24,16},{28,20},{1,9},{5... | collective-permute-start | bytes 245768 | tf_op jit(solution)/shard_map/ppermute | solution.py:453
  54.4 6.3 %collective-permute-start.8 = (bf16[40,1024]{1,0:T(8,128)(2,1)}, bf16[40,1024]{1,0:T(8,128)(2,1)S(1)}, u32[]{:S(2)}, u32[]{:S(2)}) collective-permute-start(bf16[40,1024]{1,0:T(8,128)(2,1)} %get-tuple-element.89.refs_0_), channel_id=1, source_target_pairs={{0,4},{4,0},{8,12},{12,8},{16,20},{20,16},{24,28},{28,24},{1,5},{5... | collective-permute-start | bytes 245768 | tf_op jit(solution)/shard_map/ppermute | solution.py:453
  54.4 6.3 %collective-permute-start.14 = (bf16[40,1024]{1,0:T(8,128)(2,1)S(1)}, bf16[40,1024]{1,0:T(8,128)(2,1)S(1)}, u32[]{:S(2)}, u32[]{:S(2)}) collective-permute-start(bf16[40,1024]{1,0:T(8,128)(2,1)S(1)} %collective-permute-done.13.refs_6_), channel_id=1, source_target_pairs={{0,4},{4,0},{8,12},{12,8},{16,20},{20,16},{24,28},{28,24},{1,5},{5... | collective-permute-start | bytes 245768 | tf_op jit(solution)/shard_map/ppermute | solution.py:455
  55.5 5.2 %collective-permute-start.12 = (bf16[40,1024]{1,0:T(8,128)(2,1)S(1)}, bf16[40,1024]{1,0:T(8,128)(2,1)S(1)}, u32[]{:S(2)}, u32[]{:S(2)}) collective-permute-start(bf16[40,1024]{1,0:T(8,128)(2,1)S(1)} %collective-permute-done.11.refs_4_), channel_id=1, source_target_pairs={{0,4},{4,0},{8,12},{12,8},{16,20},{20,16},{24,28},{28,24},{1,5},{5... | collective-permute-start | bytes 245768 | tf_op jit(solution)/shard_map/ppermute | solution.py:455
  57.6 3.2 %collective-permute-start.10 = (bf16[40,1024]{1,0:T(8,128)(2,1)S(1)}, bf16[40,1024]{1,0:T(8,128)(2,1)S(1)}, u32[]{:S(2)}, u32[]{:S(2)}) collective-permute-start(bf16[40,1024]{1,0:T(8,128)(2,1)S(1)} %collective-permute-done.9.refs_2_), channel_id=1, source_target_pairs={{0,4},{4,0},{8,12},{12,8},{16,20},{20,16},{24,28},{28,24},{1,5},{5... | collective-permute-start | bytes 245768 | tf_op jit(solution)/shard_map/ppermute | solution.py:455
  57.6 3.2 %copy-start.1 = (bf16[256,512]{1,0:T(8,128)(2,1)S(1)}, bf16[256,512]{1,0:T(8,128)(2,1)}, u32[]{:S(2)}) copy-start(bf16[256,512]{1,0:T(8,128)(2,1)} %get-tuple-element.90.refs_8_) | copy-start | bytes 786436
  57.6 3.2 %copy-start.3 = (bf16[40,1024]{1,0:T(8,128)(2,1)S(1)}, bf16[40,1024]{1,0:T(8,128)(2,1)}, u32[]{:S(2)}) copy-start(bf16[40,1024]{1,0:T(8,128)(2,1)} %get-tuple-element.89.refs_0_) | copy-start | bytes 245764
